TPU v7x, 128 devices: a whole 4x4x4 slice. The times are simulated.
128 devices in a mesh: wide: 32 (over y, z, core), narrow: 4 (over x).
Axes of the slice: x: 4, y: 4, z: 4, core: 2. Of those that a mesh axis runs over, the one named last changes fastest.
Arguments:
- charges: float32 [2, 8388608], P(None, ('wide', 'narrow')), may hold values from -6 to 6
- source_order: int32 [8388608], P(('wide', 'narrow')), may hold values from 0 to 7, as said below
- velocity: bfloat16 [1048576], P(('wide', 'narrow')), may hold values from 0.5 to 4
- leaf_weight: bfloat16 [16, 128], replicated, may hold values from -1.5 to 1.5
- mixing: bfloat16 [10, 2, 2, 128, 128], replicated, may hold values from -0.375 to 0.375
- eval_weight: bfloat16 [128, 16], replicated, may hold values from -0.5 to 0.5
- target_order: int32 [8388608], P(('wide', 'narrow')), may hold values from 0 to 7, as said below
Outputs:
- potentials: float32 [2, 8388608], P(None, ('wide', 'narrow'))
Inputs may be any that keep to these rules, and one draw needn't show every extreme that they name: `source_order`: each aligned block of 8 entries is a permutation of 0 .. 7. `target_order`: each aligned block of 8 entries is a permutation of 0 .. 7.
All inputs are finite; a program needn't handle non-finite values.
Results may differ from a plain program's by a relative error of at most 0.02.
Values may be sent and summed in bfloat16 or wider, within the bound.
A program may use at most 128 MiB of HBM per device.

v0:
```python
import math

import jax
import jax.numpy as jnp
from jax import lax
from jax.sharding import PartitionSpec as P

LOCAL_LEVELS = 3


def from_partner(block, axis, distance):
    count = lax.axis_size(axis)
    route = []
    for low in range(count):
        high = low | 1 << distance
        if high != low and high < count:
            route += [(low, high), (high, low)]
    return lax.ppermute(block, axis, route)


def rotate(pre, speeds, section_no):
    rank = pre.shape[1] // 2
    nodes = jnp.cos(math.pi * (jnp.arange(rank, dtype=jnp.float32) + 0.5) / rank)
    theta = math.pi * (section_no + 1) * speeds.astype(jnp.float32)[:, None] * nodes[None, :]
    cosine = jnp.cos(theta)
    sine = jnp.sin(theta)
    real_part = pre[:, :rank]
    imag_part = pre[:, rank:]
    return jnp.concatenate(
        [real_part * cosine - imag_part * sine, real_part * sine + imag_part * cosine], axis=1
    ).astype(jnp.bfloat16)


def butterfly_section(state, speeds, mixing, section_no, stride):
    total, width = state.shape
    blocks = state.reshape(total // (2 * stride), 2, stride, width)
    first = blocks[:, 0].reshape(-1, width)
    second = blocks[:, 1].reshape(-1, width)
    results = []
    for target in range(2):
        pre = jnp.dot(first, mixing[section_no, target, 0], preferred_element_type=jnp.float32)
        pre = pre + jnp.dot(
            second, mixing[section_no, target, 1], preferred_element_type=jnp.float32
        )
        results.append(pre.reshape(total // (2 * stride), stride, width))
    pre = jnp.stack(results, axis=1).reshape(total, width)
    return rotate(pre, speeds, section_no)


def combine_pair(own_part, far_part, bit_value, speeds, mixing, section_no):
    section_maps = mixing[section_no]
    pre = jnp.dot(own_part, section_maps[bit_value, bit_value], preferred_element_type=jnp.float32)
    pre = pre + jnp.dot(
        far_part, section_maps[bit_value, 1 - bit_value], preferred_element_type=jnp.float32
    )
    return rotate(pre, speeds, section_no)


def pick_within_box(source_rows, order_rows):
    leaf_size = source_rows.shape[-1]
    picked = jnp.zeros(source_rows.shape, jnp.float32)
    for slot_no in range(leaf_size):
        picked = picked + jnp.where(
            order_rows[None] == slot_no, source_rows[..., slot_no : slot_no + 1], 0.0
        )
    return picked


def on_device(charges, source_order, velocity, leaf_weight, mixing, eval_weight, target_order):
    leaf_size = leaf_weight.shape[0] // 2
    box_count = charges.shape[1] // leaf_size
    charge_rows = charges.reshape(2, box_count, leaf_size)
    ordered = pick_within_box(charge_rows, source_order.reshape(box_count, leaf_size))
    leaf_in = ordered.transpose(1, 0, 2).reshape(box_count, 2 * leaf_size).astype(jnp.bfloat16)
    state = jnp.dot(leaf_in, leaf_weight, preferred_element_type=jnp.float32).astype(jnp.bfloat16)
    for section_no in range(LOCAL_LEVELS):
        state = butterfly_section(state, velocity, mixing, section_no, 2**section_no)
    section_base = LOCAL_LEVELS
    narrow_bits = lax.axis_size("narrow").bit_length() - 1
    wide_bits = lax.axis_size("wide").bit_length() - 1
    for bit_no in range(narrow_bits):
        far_part = from_partner(state, "narrow", bit_no)
        bit_value = lax.axis_index("narrow") >> bit_no & 1
        state = combine_pair(state, far_part, bit_value, velocity, mixing, section_base + bit_no)
    section_base = section_base + narrow_bits
    for bit_no in range(wide_bits):
        far_part = from_partner(state, "wide", bit_no)
        bit_value = lax.axis_index("wide") >> bit_no & 1
        state = combine_pair(state, far_part, bit_value, velocity, mixing, section_base + bit_no)
    values = jnp.dot(state, eval_weight, preferred_element_type=jnp.float32)
    field_rows = values.reshape(box_count, 2, leaf_size).transpose(1, 0, 2)
    picked = pick_within_box(field_rows, target_order.reshape(box_count, leaf_size))
    return picked.reshape(2, box_count * leaf_size)


def solution(mesh):
    return jax.shard_map(
        on_device,
        mesh=mesh,
        in_specs=(
            P(None, ("wide", "narrow")),
            P(("wide", "narrow")),
            P(("wide", "narrow")),
            P(),
            P(),
            P(),
            P(("wide", "narrow")),
        ),
        out_specs=P(None, ("wide", "narrow")),
        check_vma=False,
    )
```

profile of v0, /device:TPU:1, one launch (start us, length us, event | category | flops | bytes accessed | tf_op | source)
XLA Modules:
  0.0 693.8 jit_solution(4856435265342963882)
XLA Ops:
  0.0 9.3 %reshape.263 = f32[2,8192,8]{2,1,0:T(8,128)} reshape(f32[2,65536]{1,0:T(2,128)} %param.7) | data formatting | bytes 1048576 | tf_op jit(solution)/shard_map/reshape | solution.py:72
  9.3 45.4 %slice_reduce_fusion.7 = (f32[2,8192]{1,0:T(2,128)S(1)}, f32[2,8192]{1,0:T(2,128)S(1)}, f32[2,8192]{1,0:T(2,128)S(1)}, f32[2,8192]{1,0:T(2,128)S(1)}, f32[2,8192...) fusion(f32[2,8192,8]{2,1,0:T(8,128)} %reshape.263), kind=kLoop, calls=%fused_computation.16 | loop fusion | bytes 1048576 | tf_op jit(solution)/shard_map/slice | solution.py:64
  93.8 15.6 %copy.28 = f32[4096,2,1,128]{3,1,0,2:T(2,128)S(1)} copy(f32[4096,2,1,128]{3,0,2,1:T(8,128)S(1)} %pad_maximum_fusion) | data formatting | bytes 8388608 | tf_op jit(solution)/shard_map/stack | solution.py:46
  121.4 10.1 %fusion.81 = (bf16[8192,64]{0,1:T(8,128)(2,1)S(1)}, bf16[8192,64]{0,1:T(8,128)(2,1)}) fusion(f32[8192,64]{0,1:T(8,128)S(1)} %copy.53, f32[8192,64]{0,1:T(8,128)} %copy.54, f32[64]{0:T(128)S(1)} %multiply_cosine_fusion.10, f32[8192]{0:T(1024)S(1)} %get-tuple-element.85), kind=kLoop, calls=%fused_computation.127 | loop fusion | flops 4718592 | bytes 6324480 | tf_op jit(solution)/shard_map/convert.22
  135.5 6.8 pad_maximum_fusion.11
  160.3 10.1 %fusion.77 = (bf16[8192,64]{0,1:T(8,128)(2,1)S(1)}, bf16[8192,64]{0,1:T(8,128)(2,1)}) fusion(f32[8192,64]{0,1:T(8,128)S(1)} %copy.55, f32[8192,64]{0,1:T(8,128)} %copy.56, f32[8192]{0:T(1024)S(1)} %get-tuple-element.77, f32[64]{0:T(128)S(1)} %multiply_cosine_fusion.10), kind=kLoop, calls=%fused_computation.123 | loop fusion | flops 4718592 | bytes 6324480 | tf_op jit(solution)/shard_map/convert.18
  193.7 9.5 %fusion.71 = (bf16[8192,64]{0,1:T(8,128)(2,1)S(1)}, bf16[8192,64]{0,1:T(8,128)(2,1)S(1)}) fusion(f32[8192,64]{0,1:T(8,128)} %copy.58, f32[8192,64]{0,1:T(8,128)} %copy.57, f32[8192]{0:T(1024)S(1)} %get-tuple-element.78, f32[64]{0:T(128)S(1)} %multiply_cosine_fusion.10), kind=kLoop, calls=%fused_computation.117 | loop fusion | flops 4718592 | bytes 6324480 | tf_op jit(solution)/shard_map/convert.14
  208.4 43.5 %collective-permute-done = bf16[8192,128]{0,1:T(8,128)(2,1)} collective-permute-done((bf16[8192,128]{0,1:T(8,128)(2,1)}, bf16[8192,128]{0,1:T(8,128)(2,1)}, u32[]{:S(2)}, u32[]{:S(2)}) %collective-permute-start) | collective-permute-done | bytes 2097184 | tf_op jit(solution)/shard_map/ppermute | solution.py:18
  254.3 8.4 %fusion.67 = (bf16[8192,64]{0,1:T(8,128)(2,1)S(1)}, bf16[8192,64]{0,1:T(8,128)(2,1)S(1)}) fusion(f32[8192,128]{0,1:T(8,128)S(1)} %convolution_add_fusion.6, f32[8192]{0:T(1024)S(1)} %copy-done.18, f32[64]{0:T(128)S(1)} %multiply_cosine_fusion.10), kind=kLoop, calls=%fused_computation.113 | loop fusion | flops 4718592 | bytes 6324480 | tf_op jit(solution)/shard_map/convert.12
  268.3 43.7 %collective-permute-done.1 = bf16[8192,128]{0,1:T(8,128)(2,1)} collective-permute-done((bf16[8192,128]{0,1:T(8,128)(2,1)}, bf16[8192,128]{0,1:T(8,128)(2,1)}, u32[]{:S(2)}, u32[]{:S(2)}) %collective-permute-start.1) | collective-permute-done | bytes 2097184 | tf_op jit(solution)/shard_map/ppermute | solution.py:18
  314.4 8.4 %fusion.63 = (bf16[8192,64]{0,1:T(8,128)(2,1)S(1)}, bf16[8192,64]{0,1:T(8,128)(2,1)S(1)}) fusion(f32[8192,128]{0,1:T(8,128)S(1)} %convolution_add_fusion.5, f32[8192]{0:T(1024)S(1)} %copy-done.17, f32[64]{0:T(128)S(1)} %multiply_cosine_fusion.10), kind=kLoop, calls=%fused_computation.109 | loop fusion | flops 4718592 | bytes 6324480 | tf_op jit(solution)/shard_map/convert.10
  333.5 8.4 %fusion.59 = (bf16[8192,64]{0,1:T(8,128)(2,1)S(1)}, bf16[8192,64]{0,1:T(8,128)(2,1)S(1)}) fusion(f32[8192,128]{0,1:T(8,128)S(1)} %convolution_add_fusion.4, f32[8192]{0:T(1024)S(1)} %copy-done.16, f32[64]{0:T(128)S(1)} %multiply_cosine_fusion.10), kind=kLoop, calls=%fused_computation.105 | loop fusion | flops 4718592 | bytes 6324480 | tf_op jit(solution)/shard_map/convert.8
  346.0 45.2 %collective-permute-done.3 = bf16[8192,128]{0,1:T(8,128)(2,1)} collective-permute-done((bf16[8192,128]{0,1:T(8,128)(2,1)}, bf16[8192,128]{0,1:T(8,128)(2,1)}, u32[]{:S(2)}, u32[]{:S(2)}) %collective-permute-start.3) | collective-permute-done | bytes 2097184 | tf_op jit(solution)/shard_map/ppermute | solution.py:18
  393.7 8.4 %fusion.55 = (bf16[8192,64]{0,1:T(8,128)(2,1)S(1)}, bf16[8192,64]{0,1:T(8,128)(2,1)S(1)}) fusion(f32[8192,128]{0,1:T(8,128)S(1)} %convolution_add_fusion.3, f32[8192]{0:T(1024)S(1)} %copy-done.15, f32[64]{0:T(128)S(1)} %multiply_cosine_fusion.10), kind=kLoop, calls=%fused_computation.101 | loop fusion | flops 4718592 | bytes 6324480 | tf_op jit(solution)/shard_map/convert.6
  407.4 44.3 %collective-permute-done.4 = bf16[8192,128]{0,1:T(8,128)(2,1)} collective-permute-done((bf16[8192,128]{0,1:T(8,128)(2,1)}, bf16[8192,128]{0,1:T(8,128)(2,1)}, u32[]{:S(2)}, u32[]{:S(2)}) %collective-permute-start.4) | collective-permute-done | bytes 2097184 | tf_op jit(solution)/shard_map/ppermute | solution.py:18
  454.1 8.4 %fusion.51 = (bf16[8192,64]{0,1:T(8,128)(2,1)S(1)}, bf16[8192,64]{0,1:T(8,128)(2,1)S(1)}) fusion(f32[8192,128]{0,1:T(8,128)S(1)} %convolution_add_fusion.2, f32[8192]{0:T(1024)S(1)} %copy-done.14, f32[64]{0:T(128)S(1)} %multiply_cosine_fusion.10), kind=kLoop, calls=%fused_computation.97 | loop fusion | flops 4718592 | bytes 6324480 | tf_op jit(solution)/shard_map/convert.4
  466.1 43.6 %collective-permute-done.5 = bf16[8192,128]{0,1:T(8,128)(2,1)} collective-permute-done((bf16[8192,128]{0,1:T(8,128)(2,1)}, bf16[8192,128]{0,1:T(8,128)(2,1)}, u32[]{:S(2)}, u32[]{:S(2)}) %collective-permute-start.5) | collective-permute-done | bytes 2097184 | tf_op jit(solution)/shard_map/ppermute | solution.py:18
  512.1 8.4 %fusion.47 = (bf16[8192,64]{0,1:T(8,128)(2,1)S(1)}, bf16[8192,64]{0,1:T(8,128)(2,1)S(1)}) fusion(f32[8192,128]{0,1:T(8,128)S(1)} %convolution_add_fusion.1, f32[8192]{0:T(1024)S(1)} %copy-done.13, f32[64]{0:T(128)S(1)} %multiply_cosine_fusion.10), kind=kLoop, calls=%fused_computation.93 | loop fusion | flops 4718592 | bytes 6324480 | tf_op jit(solution)/shard_map/convert.2
  527.0 41.5 %collective-permute-done.6 = bf16[8192,128]{0,1:T(8,128)(2,1)} collective-permute-done((bf16[8192,128]{0,1:T(8,128)(2,1)}, bf16[8192,128]{0,1:T(8,128)(2,1)}, u32[]{:S(2)}, u32[]{:S(2)}) %collective-permute-start.6) | collective-permute-done | bytes 2097184 | tf_op jit(solution)/shard_map/ppermute | solution.py:18
  571.0 8.4 %fusion.43 = (bf16[8192,64]{0,1:T(8,128)(2,1)S(1)}, bf16[8192,64]{0,1:T(8,128)(2,1)S(1)}) fusion(f32[8192,128]{0,1:T(8,128)S(1)} %convolution_add_fusion, f32[8192]{0:T(1024)S(1)} %copy-done.12, f32[64]{0:T(128)S(1)} %multiply_cosine_fusion.10), kind=kLoop, calls=%fused_computation.89 | loop fusion | flops 4718592 | bytes 6324480 | tf_op jit(solution)/shard_map/convert
  586.3 7.7 %broadcast_in_dim.307 = f32[2,65536]{1,0:T(2,128)S(1)} reshape(f32[2,8192,8]{2,1,0:T(8,128)} %broadcast_in_dim.306) | data formatting | bytes 1048576 | tf_op jit(solution)/shard_map/jit(_where)/broadcast_in_dim | solution.py:63
  594.0 5.7 broadcast_in_dim.311
  599.7 7.7 %broadcast_in_dim.312 = f32[2,65536]{1,0:T(2,128)S(1)} reshape(f32[2,8192,8]{2,1,0:T(8,128)} %broadcast_in_dim.311) | data formatting | bytes 1048576 | tf_op jit(solution)/shard_map/jit(_where)/broadcast_in_dim | solution.py:63
  612.9 7.7 %broadcast_in_dim.316 = f32[2,65536]{1,0:T(2,128)S(1)} reshape(f32[2,8192,8]{2,1,0:T(8,128)} %broadcast_in_dim.315) | data formatting | bytes 1048576 | tf_op jit(solution)/shard_map/jit(_where)/broadcast_in_dim | solution.py:63
  620.6 5.5 broadcast_in_dim.319
  626.1 7.7 %broadcast_in_dim.320 = f32[2,65536]{1,0:T(2,128)S(1)} reshape(f32[2,8192,8]{2,1,0:T(8,128)} %broadcast_in_dim.319) | data formatting | bytes 1048576 | tf_op jit(solution)/shard_map/jit(_where)/broadcast_in_dim | solution.py:63
  639.2 7.7 %broadcast_in_dim.324 = f32[2,65536]{1,0:T(2,128)S(1)} reshape(f32[2,8192,8]{2,1,0:T(8,128)} %broadcast_in_dim.323) | data formatting | bytes 1048576 | tf_op jit(solution)/shard_map/jit(_where)/broadcast_in_dim | solution.py:63
  646.9 5.5 broadcast_in_dim.327
  652.4 7.7 %broadcast_in_dim.328 = f32[2,65536]{1,0:T(2,128)S(1)} reshape(f32[2,8192,8]{2,1,0:T(8,128)} %broadcast_in_dim.327) | data formatting | bytes 1048576 | tf_op jit(solution)/shard_map/jit(_where)/broadcast_in_dim | solution.py:63
  666.4 8.6 %broadcast_in_dim.332 = f32[2,65536]{1,0:T(2,128)} reshape(f32[2,8192,8]{2,1,0:T(8,128)} %broadcast_in_dim.331) | data formatting | bytes 1048576 | tf_op jit(solution)/shard_map/jit(_where)/broadcast_in_dim | solution.py:63
  675.0 5.5 broadcast_in_dim.335
  680.5 8.5 %broadcast_in_dim.336 = f32[2,65536]{1,0:T(2,128)} reshape(f32[2,8192,8]{2,1,0:T(8,128)} %broadcast_in_dim.335) | data formatting | bytes 1048576 | tf_op jit(solution)/shard_map/jit(_where)/broadcast_in_dim | solution.py:63
  (134 shorter events, 179.6 us)
Async XLA Ops:
  0.0 84.9 %copy-start = (bf16[16,128]{1,0:T(8,128)(2,1)S(1)}, bf16[16,128]{1,0:T(8,128)(2,1)}, u32[]{:S(2)}) copy-start(bf16[16,128]{1,0:T(8,128)(2,1)} %param.10) | copy-start | bytes 12292
  9.3 45.4 %copy-start.10 = (s32[65536]{0:T(1024)S(1)}, s32[65536]{0:T(1024)}, u32[]{:S(2)}) copy-start(s32[65536]{0:T(1024)} %param.8) | copy-start | bytes 786436
  116.9 3.9 copy-start.19
  174.2 4.6 copy-start.2
  204.7 47.2 %collective-permute-start = (bf16[8192,128]{0,1:T(8,128)(2,1)}, bf16[8192,128]{0,1:T(8,128)(2,1)}, u32[]{:S(2)}, u32[]{:S(2)}) collective-permute-start(bf16[8192,128]{0,1:T(8,128)(2,1)} %pad_maximum_fusion.3), channel_id=1, source_target_pairs={{0,1},{1,0},{2,3},{3,2},{4,5},{5,4},{6,7},{7,6},{8,9},{9,8},{10,11... | collective-permute-start | bytes 6291464 | tf_op jit(solution)/shard_map/ppermute | solution.py:18
  208.4 46.0 %copy-start.18 = (f32[8192]{0:T(1024)S(1)}, f32[8192]{0:T(1024)}, u32[]{:S(2)}) copy-start(f32[8192]{0:T(1024)} %get-tuple-element.79) | copy-start | bytes 98308
  262.8 4.7 copy-start.7
  264.3 47.7 %collective-permute-start.1 = (bf16[8192,128]{0,1:T(8,128)(2,1)}, bf16[8192,128]{0,1:T(8,128)(2,1)}, u32[]{:S(2)}, u32[]{:S(2)}) collective-permute-start(bf16[8192,128]{0,1:T(8,128)(2,1)} %pad_maximum_fusion.4), channel_id=1, source_target_pairs={{0,2},{2,0},{1,3},{3,1},{4,6},{6,4},{5,7},{7,5},{8,10},{10,8},{9,1... | collective-permute-start | bytes 6291464 | tf_op jit(solution)/shard_map/ppermute | solution.py:18
  268.3 46.2 %copy-start.17 = (f32[8192]{0:T(1024)S(1)}, f32[8192]{0:T(1024)}, u32[]{:S(2)}) copy-start(f32[8192]{0:T(1024)} %get-tuple-element.80) | copy-start | bytes 98308
  322.9 4.1 copy-start.6
  324.4 6.7 collective-permute-start.2
  327.7 5.8 copy-start.16
  341.9 3.3 copy-start.5
  343.4 47.8 %collective-permute-start.3 = (bf16[8192,128]{0,1:T(8,128)(2,1)}, bf16[8192,128]{0,1:T(8,128)(2,1)}, u32[]{:S(2)}, u32[]{:S(2)}) collective-permute-start(bf16[8192,128]{0,1:T(8,128)(2,1)} %pad_maximum_fusion.6), channel_id=1, source_target_pairs={{0,8},{8,0},{4,12},{12,4},{16,24},{24,16},{20,28},{28,20},{32,40},... | collective-permute-start | bytes 6291464 | tf_op jit(solution)/shard_map/ppermute | solution.py:18
  346.0 47.7 %copy-start.15 = (f32[8192]{0:T(1024)S(1)}, f32[8192]{0:T(1024)}, u32[]{:S(2)}) copy-start(f32[8192]{0:T(1024)} %get-tuple-element.82) | copy-start | bytes 98308
  402.1 4.6 copy-start.4
  403.6 48.1 %collective-permute-start.4 = (bf16[8192,128]{0,1:T(8,128)(2,1)}, bf16[8192,128]{0,1:T(8,128)(2,1)}, u32[]{:S(2)}, u32[]{:S(2)}) collective-permute-start(bf16[8192,128]{0,1:T(8,128)(2,1)} %pad_maximum_fusion.7), channel_id=1, source_target_pairs={{0,16},{16,0},{4,20},{20,4},{8,24},{24,8},{12,28},{28,12},{32,48},... | collective-permute-start | bytes 6291464 | tf_op jit(solution)/shard_map/ppermute | solution.py:18
  407.4 46.7 %copy-start.14 = (f32[8192]{0:T(1024)S(1)}, f32[8192]{0:T(1024)}, u32[]{:S(2)}) copy-start(f32[8192]{0:T(1024)} %get-tuple-element.83) | copy-start | bytes 98308
  462.6 2.8 copy-start.3
  464.1 45.6 %collective-permute-start.5 = (bf16[8192,128]{0,1:T(8,128)(2,1)}, bf16[8192,128]{0,1:T(8,128)(2,1)}, u32[]{:S(2)}, u32[]{:S(2)}) collective-permute-start(bf16[8192,128]{0,1:T(8,128)(2,1)} %pad_maximum_fusion.8), channel_id=1, source_target_pairs={{0,32},{32,0},{4,36},{36,4},{8,40},{40,8},{12,44},{44,12},{16,48},... | collective-permute-start | bytes 6291464 | tf_op jit(solution)/shard_map/ppermute | solution.py:18
  466.1 46.0 %copy-start.13 = (f32[8192]{0:T(1024)S(1)}, f32[8192]{0:T(1024)}, u32[]{:S(2)}) copy-start(f32[8192]{0:T(1024)} %get-tuple-element.84) | copy-start | bytes 98308
  520.6 4.7 copy-start.11
  522.1 46.5 %collective-permute-start.6 = (bf16[8192,128]{0,1:T(8,128)(2,1)}, bf16[8192,128]{0,1:T(8,128)(2,1)}, u32[]{:S(2)}, u32[]{:S(2)}) collective-permute-start(bf16[8192,128]{0,1:T(8,128)(2,1)} %pad_maximum_fusion.9), channel_id=1, source_target_pairs={{0,64},{64,0},{4,68},{68,4},{8,72},{72,8},{12,76},{76,12},{16,80},... | collective-permute-start | bytes 6291464 | tf_op jit(solution)/shard_map/ppermute | solution.py:18
  527.0 44.0 %copy-start.12 = (f32[8192]{0:T(1024)S(1)}, f32[8192]{0:T(1024)}, u32[]{:S(2)}) copy-start(f32[8192]{0:T(1024)} %get-tuple-element.76) | copy-start | bytes 98308
  571.0 8.4 %copy-start.20 = (bf16[128,16]{0,1:T(8,128)(2,1)S(1)}, bf16[128,16]{0,1:T(8,128)(2,1)}, u32[]{:S(2)}) copy-start(bf16[128,16]{0,1:T(8,128)(2,1)} %param.12) | copy-start | bytes 12292
  680.5 8.6 %copy-start.8 = (pred[65536]{0:T(1024)(128)(4,1)S(1)}, pred[65536]{0:T(1024)(128)(4,1)}, u32[]{:S(2)}) copy-start(pred[65536]{0:T(1024)(128)(4,1)} %get-tuple-element.64) | copy-start | bytes 196612
  680.5 8.5 %copy-start.9 = (pred[65536]{0:T(1024)(128)(4,1)S(1)}, pred[65536]{0:T(1024)(128)(4,1)}, u32[]{:S(2)}) copy-start(pred[65536]{0:T(1024)(128)(4,1)} %get-tuple-element.65) | copy-start | bytes 196612
  689.0 4.5 copy-start.1
where the time goes:
time: 701 us; the launch traced here: 694 us
  waiting for transfers between devices  265 us (38%)
  local copies, waits for them, and re-layouts  256 us (37%)
  other arithmetic  120 us (17%)
  matrix products  34.4 us (5%)
  starting transfers between devices  17.1 us (2%)
    ppermute x7, waiting for transfers between devices, from_partner(): return lax.ppermute(block, axis, route)  265 us
    broadcast_in_dim x16, local copies, waits for them, and re-layouts, pick_within_box(): jnp.where(order_rows[None] == slot_no, source_rows[..., slot_no:slot_no +...  107 us
    another operation x10, other arithmetic  88.7 us
    slice x2, local copies, waits for them, and re-layouts, pick_within_box(): source_rows[..., slot_no:slot_no + 1]  46.5 us
    eq x16, local copies, waits for them, and re-layouts, pick_within_box(): order_rows[None] == slot_no  29.8 us
    unnamed x52, local copies, waits for them, and re-layouts  22.4 us
    concatenate x9, other arithmetic, rotate(): jnp.concatenate([real_part * cosine - imag_part * sine, real_part * sine...  21.9 us
    ppermute x7, starting transfers between devices, from_partner(): return lax.ppermute(block, axis, route)  17.1 us
  transfers between devices with their start and end apart: 7, of which 7 were waited for; matrix products, arithmetic and copies ran while one was open for 1% of the time, Pallas kernels for 0%

commit v1 on v0

v1 whole, which is shorter than its diff:
```python
import functools
import math

import jax
import jax.numpy as jnp
import numpy as np
from jax import lax
from jax.experimental import pallas as pl
from jax.experimental.pallas import tpu as pltpu
from jax.sharding import PartitionSpec as P

MESH = pl.DeviceIdType.MESH
LEVELS = 10
PARTS = 128
E = 8
B = 8
W = 128
VMEM = pl.BlockSpec(memory_space=pltpu.VMEM)


def half_sine_terms(count):
    w = 0.125 * (1 + np.cos(np.pi * (np.arange(64) + 0.5) / 64))
    u = np.sqrt(w)
    target = math.sqrt(2) * np.sin(np.pi * u) / u
    return np.polynomial.polynomial.polyfit(w, target, count - 1)


def phase_map():
    rank = W // 2
    nodes = np.cos(np.float32(math.pi) * (np.arange(rank, dtype=np.float32) + np.float32(0.5)) / np.float32(rank))
    rest = np.tile(nodes.astype(np.float64) * 0.5, 2)
    out = np.zeros((4, E, B, B, W), np.float64)
    for piece in range(3):
        part = rest.astype(jnp.bfloat16).astype(np.float64)
        rest = rest - part
        for b in range(B):
            out[piece, :, b, b, :] = part
    out[3, 0, 0, :, rank:] = -0.25
    return out.reshape(4 * E * B, B * W).astype(jnp.bfloat16)


def low_half(shape):
    return lax.broadcasted_iota(jnp.int32, shape, len(shape) - 1) % W < W // 2


def half_turn(x):
    return pltpu.roll(x, W // 2, x.ndim - 1)


def slot_of(order):
    lane = lax.broadcasted_iota(jnp.int32, order.shape, 1)
    return (lane // 8) * 8 + order


def pack_kernel(charges_ref, order_ref, out_ref):
    rows = 64
    half = PARTS // 2

    def body(step, _):
        at = pl.ds(pl.multiple_of(step * rows, rows), rows)
        index = slot_of(order_ref[at])
        first = jnp.take_along_axis(charges_ref[0, at], index, axis=1, mode="promise_in_bounds")
        second = jnp.take_along_axis(charges_ref[1, at], index, axis=1, mode="promise_in_bounds")
        low = low_half(first.shape)
        even = jnp.where(low, first, half_turn(second)).astype(jnp.bfloat16)
        odd = jnp.where(low, half_turn(first), second).astype(jnp.bfloat16)
        out_ref[pl.ds(step * (rows // E), rows // E)] = even.reshape(rows // E, E, W)
        out_ref[pl.ds(half + step * (rows // E), rows // E)] = odd.reshape(rows // E, E, W)
        return 0

    lax.fori_loop(0, half * E // rows, body, 0)


def unpack_kernel(field_ref, order_ref, out_ref):
    rows = 64
    half = PARTS // 2

    def body(step, _):
        at = pl.ds(pl.multiple_of(step * rows, rows), rows)
        index = slot_of(order_ref[at])
        even = field_ref[pl.ds(step * (rows // E), rows // E)].astype(jnp.float32).reshape(rows, W)
        odd = field_ref[pl.ds(half + step * (rows // E), rows // E)].astype(jnp.float32).reshape(rows, W)
        low = low_half(even.shape)
        first = jnp.where(low, even, half_turn(odd))
        second = jnp.where(low, half_turn(even), odd)
        out_ref[0, at] = jnp.take_along_axis(first, index, axis=1, mode="promise_in_bounds")
        out_ref[1, at] = jnp.take_along_axis(second, index, axis=1, mode="promise_in_bounds")
        return 0

    lax.fori_loop(0, half * E // rows, body, 0)


def place(index, narrow):
    return (index // narrow, index % narrow)


def exchange_kernel(narrow, count, *refs):
    sources, targets, sends, recvs = (refs[i * count : (i + 1) * count] for i in range(4))
    me = lax.axis_index("wide") * narrow + lax.axis_index("narrow")
    barrier = pltpu.get_barrier_semaphore()

    def greet(k, _):
        pl.semaphore_signal(barrier, inc=1, device_id=place(me ^ k, narrow), device_id_type=MESH)
        return 0

    lax.fori_loop(1, PARTS, greet, 0)
    pl.semaphore_wait(barrier, PARTS - 1)

    def send(k, _):
        to = me ^ k
        for i in reversed(range(count)):
            pltpu.make_async_remote_copy(
                sources[i].at[to], targets[i].at[me], sends[i], recvs[i],
                device_id=place(to, narrow), device_id_type=MESH,
            ).start()
        return 0

    lax.fori_loop(1, PARTS, send, 0)
    for i in range(count):
        targets[i][me] = sources[i][me]
    others = pl.ds(0, PARTS - 1)
    for i in range(count):
        for sem in (recvs[i], sends[i]):
            pltpu.make_async_copy(sources[i].at[others], targets[i].at[others], sem).wait()


def exchange(narrow, arrays, collective_id):
    count = len(arrays)
    return pl.pallas_call(
        functools.partial(exchange_kernel, narrow, count),
        out_shape=tuple(jax.ShapeDtypeStruct(a.shape, a.dtype) for a in arrays),
        in_specs=[VMEM] * count,
        out_specs=(VMEM,) * count,
        scratch_shapes=[pltpu.SemaphoreType.DMA] * (2 * count),
        compiler_params=pltpu.CompilerParams(has_side_effects=True, collective_id=collective_id),
    )(*arrays)


def rotate(pre, turn):
    low = low_half(turn.shape)
    other = half_turn(turn)
    cosine = jnp.where(low, turn, other)
    sine = jnp.where(low, -other, turn)
    return pre * cosine + half_turn(pre) * sine


def level_map(mixing_ref, level):
    return jnp.concatenate(
        [jnp.concatenate([mixing_ref[level, j, i] for i in range(2)], axis=0) for j in range(2)], axis=1
    )


def pair_up(even, odd):
    rows = even.shape[0]
    both = jnp.concatenate([even.reshape(rows // E, E, W), odd.reshape(rows // E, E, W)], axis=1)
    return both.reshape(2 * rows, W)


def levels_kernel(
    leaf_ref, speed_ref, leaf_map_ref, mixing_ref, eval_map_ref, phase_ref, out_ref, state, turn_p, turn_q
):
    terms = half_sine_terms(5)
    early = {0: 0, 1: 1, 9: 2}

    nd = 8

    def turns(step, _):
        rows = nd * E
        at = pl.ds(pl.multiple_of(step * nd, nd), nd)
        speeds = jnp.broadcast_to(speed_ref[at].astype(jnp.float32), (nd, E, W)).reshape(rows, W)
        lane = lax.broadcasted_iota(jnp.int32, (rows, W), 1)
        row = lax.broadcasted_iota(jnp.int32, (rows, W), 0)
        own = jnp.where((lane % 64) // B == row % E, speeds, 0.0)
        tail = jnp.where(lane < 64, own, jnp.where(lane == 64, 1.0, 0.0))
        operand = jnp.concatenate([own, tail], axis=1).astype(jnp.bfloat16)
        turn_count = jnp.dot(operand, phase_ref[...], preferred_element_type=jnp.float32)
        low = low_half((rows, W))
        rows_at = pl.ds(pl.multiple_of(step * rows, rows), rows)
        wide_at = pl.ds(pl.multiple_of(step * rows * 2, rows * 2), rows * 2)
        for pair in range(B // 2):
            now, before, twice = [], [], []
            for b in (2 * pair, 2 * pair + 1):
                u = turn_count[:, b * W : (b + 1) * W]
                u = u - jnp.round(u)
                w = u * u
                p = jnp.float32(terms[4])
                for k in (3, 2, 1, 0):
                    p = p * w + jnp.float32(terms[k])
                s = u * p
                t = 1.0 - s * s
                now.append(t)
                before.append(jnp.where(low, 1.0, 0.0))
                c = jnp.where(low, t, half_turn(t))
                twice.append(c + c)
            for level in range(LEVELS):
                if level in early:
                    for i in range(2):
                        turn_p[early[level], 2 * pair + i, rows_at] = now[i].astype(jnp.bfloat16)
                else:
                    turn_q[level - 2, pair, wide_at] = pair_up(now[0], now[1]).astype(jnp.bfloat16)
                if level < LEVELS - 1:
                    now, before = [twice[i] * now[i] - before[i] for i in range(2)], now
        return 0

    lax.fori_loop(0, PARTS // nd, turns, 0)

    nl = 16

    def first_levels(step, _):
        rows = nl * E
        at = pl.ds(pl.multiple_of(step * nl, nl), nl)
        rows_at = pl.ds(pl.multiple_of(step * rows, rows), rows)
        wide_at = pl.ds(pl.multiple_of(step * rows * 2, rows * 2), rows * 2)
        leaf = leaf_ref[at].reshape(rows, W)
        spread = jnp.dot(leaf, leaf_map_ref[...], preferred_element_type=jnp.float32).astype(jnp.bfloat16)
        boxes = [spread[:, b * W : (b + 1) * W] for b in range(B)]
        for level in range(3):
            maps = level_map(mixing_ref, level)
            pres = [None] * B
            for b in range(B):
                if b >> level & 1:
                    continue
                far = b | 1 << level
                pre = jnp.dot(
                    jnp.concatenate([boxes[b], boxes[far]], axis=1), maps, preferred_element_type=jnp.float32
                )
                pres[b], pres[far] = pre[:, :W], pre[:, W:]
            if level < 2:
                boxes = [
                    rotate(pres[b].astype(jnp.bfloat16), turn_p[early[level], b, rows_at]) for b in range(B)
                ]
            else:
                for pair in range(B // 2):
                    pre = pair_up(pres[2 * pair], pres[2 * pair + 1]).astype(jnp.bfloat16)
                    state[pair, wide_at] = rotate(pre, turn_q[0, pair, wide_at])
        return 0

    lax.fori_loop(0, PARTS // nl, first_levels, 0)

    for level in range(3, LEVELS - 1):
        stride = 2 * E << (level - 3)
        block = min(stride, 512)
        per = stride // block
        group = 512 // block
        maps = level_map(mixing_ref, level)
        steps_of_pair = PARTS * 2 * E // (2 * block * group)

        def later(step, _, level=level, stride=stride, block=block, per=per, group=group, maps=maps):
            pair = step // steps_of_pair
            inner = step % steps_of_pair
            near, far = [], []
            for g in range(group):
                unit = inner * group + g
                start = (unit // per) * (2 * stride) + (unit % per) * block
                near.append(pl.ds(pl.multiple_of(start, block), block))
                far.append(pl.ds(pl.multiple_of(start + stride, block), block))
            lhs = jnp.concatenate(
                [
                    jnp.concatenate([state[pair, at] for at in near], axis=0),
                    jnp.concatenate([state[pair, at] for at in far], axis=0),
                ],
                axis=1,
            )
            pre = jnp.dot(lhs, maps, preferred_element_type=jnp.float32)
            for g in range(group):
                for side, at in ((0, near[g]), (1, far[g])):
                    own = pre[g * block : (g + 1) * block, side * W : (side + 1) * W].astype(jnp.bfloat16)
                    state[pair, at] = rotate(own, turn_q[level - 2, pair, at])
            return 0

        lax.fori_loop(0, (B // 2) * steps_of_pair, later, 0)

    last = LEVELS - 1
    ne = 16

    def finish(step, _):
        rows = ne * 2 * E
        maps = level_map(mixing_ref, last)
        half = PARTS * E // 2
        near = pl.ds(pl.multiple_of(step * rows, rows), rows)
        far = pl.ds(pl.multiple_of(step * rows + 2 * half, rows), rows)
        boxes = [[None] * B for _ in range(2)]
        for pair in range(B // 2):
            lhs = jnp.concatenate([state[pair, near], state[pair, far]], axis=1)
            pre = jnp.dot(lhs, maps, preferred_element_type=jnp.float32)
            for side in range(2):
                own = pre[:, side * W : (side + 1) * W].reshape(ne, 2, E, W)
                rows_at = pl.ds(pl.multiple_of(step * ne * E + side * half, ne * E), ne * E)
                for i in range(2):
                    box = own[:, i].reshape(ne * E, W).astype(jnp.bfloat16)
                    boxes[side][2 * pair + i] = rotate(box, turn_p[early[last], 2 * pair + i, rows_at])
        for side in range(2):
            values = jnp.dot(
                jnp.concatenate(boxes[side], axis=1), eval_map_ref[...], preferred_element_type=jnp.float32
            )
            at = pl.ds(step * ne + side * (PARTS // 2), ne)
            out_ref[at] = values.astype(jnp.bfloat16).reshape(ne, E, W)
        return 0

    lax.fori_loop(0, PARTS // 2 // ne, finish, 0)


def on_device(narrow, charges, source_order, velocity, leaf_weight, mixing, eval_weight, target_order):
    lines = charges.shape[1] // W
    eye = jnp.eye(B, dtype=jnp.bfloat16)
    leaf_map = leaf_weight.reshape(2, 1, 8, 1, W) * eye.reshape(1, B, 1, B, 1)
    leaf_map = leaf_map.reshape(W, B * W)
    eval_map = eval_weight.reshape(1, W, 2, 1, 8) * eye.reshape(B, 1, 1, B, 1)
    eval_map = eval_map.reshape(B * W, W)
    half = PARTS // 2
    speeds = velocity.reshape(half, E, 2, B).transpose(2, 0, 1, 3).reshape(PARTS, 1, E * B)
    speeds = jnp.concatenate([speeds, speeds], axis=2)

    packed = pl.pallas_call(
        pack_kernel,
        out_shape=jax.ShapeDtypeStruct((PARTS, E, W), jnp.bfloat16),
        in_specs=[VMEM] * 2,
        out_specs=VMEM,
    )(charges.reshape(2, lines, W), source_order.reshape(lines, W))
    leaf, speeds = exchange(narrow, (packed, speeds), 0)
    values = pl.pallas_call(
        levels_kernel,
        out_shape=jax.ShapeDtypeStruct((PARTS, E, W), jnp.bfloat16),
        in_specs=[VMEM] * 6,
        out_specs=VMEM,
        scratch_shapes=[
            pltpu.VMEM((B // 2, PARTS * 2 * E, W), jnp.bfloat16),
            pltpu.VMEM((3, B, PARTS * E, W), jnp.bfloat16),
            pltpu.VMEM((LEVELS - 3, B // 2, PARTS * 2 * E, W), jnp.bfloat16),
        ],
        compiler_params=pltpu.CompilerParams(vmem_limit_bytes=56 * 2**20),
    )(leaf, speeds, leaf_map, mixing, eval_map, jnp.asarray(phase_map()))
    (field,) = exchange(narrow, (values,), 1)
    out = pl.pallas_call(
        unpack_kernel,
        out_shape=jax.ShapeDtypeStruct((2, lines, W), jnp.float32),
        in_specs=[VMEM] * 2,
        out_specs=VMEM,
    )(field, target_order.reshape(lines, W))
    return out.reshape(2, lines * W)


def solution(mesh):
    both = ("wide", "narrow")
    return jax.shard_map(
        functools.partial(on_device, mesh.shape["narrow"]),
        mesh=mesh,
        in_specs=(P(None, both), P(both), P(both), P(), P(), P(), P(both)),
        out_specs=P(None, both),
        check_vma=False,
    )
```

time: 701 us -> 87.9 us (0.13)
  waiting for transfers between devices: 265 us -> 0 us
  local copies, waits for them, and re-layouts: 256 us -> 5.86 us
  other arithmetic: 120 us -> 1.75 us
  Pallas kernels: 0 us -> 79.9 us
  matrix products: 34.4 us -> 0 us
  starting transfers between devices: 17.1 us -> 0 us
    ppermute x7 -> x0, waiting for transfers between devices: 265 us -> none  [from_partner(): return lax.ppermute(block, axis, route)]
    broadcast_in_dim x16 -> x0, local copies, waits for them, and re-layouts: 107 us -> none  [pick_within_box(): jnp.where(order_rows[None] == slot_no, source_rows[..., slot_no:slot_no +...]
    another operation x13 -> x0, other arithmetic: 91.8 us -> none
    pallas_call x0 -> x5, Pallas kernels: none -> 79.9 us  [the longest x2 36.8 us: exchange(): pl.pallas_call(functools.partial(exchange_kernel, narrow, count), out_sha...]
    slice x7 -> x0, local copies, waits for them, and re-layouts: 64.1 us -> none  [the longest x2 46.5 us: pick_within_box(): source_rows[..., slot_no:slot_no + 1]]
    dot_general x28 -> x0, matrix products: 34.4 us -> none  [the longest x7 16.8 us: combine_pair(): jnp.dot(far_part, section_maps[bit_value, 1 - bit_value], preferred_eleme...]
    eq x16 -> x0, local copies, waits for them, and re-layouts: 29.8 us -> none  [pick_within_box(): order_rows[None] == slot_no]
    another operation x5 -> x0, local copies, waits for them, and re-layouts: 23.5 us -> none  [the longest x1 15.6 us: butterfly_section(): pre = jnp.stack(results, axis=1).reshape(total, width)]
  transfers between devices with their start and end apart: 7 -> 0, of which waited for: 7 -> 0; matrix products, arithmetic and copies ran while one was open for 1% -> 0% of each run, Pallas kernels for 0% -> 0%
where the time goes in v1:
time: 87.9 us; the launch traced here: 87.6 us
  Pallas kernels  79.9 us (91%)
  local copies, waits for them, and re-layouts  5.86 us (7%)
  other arithmetic  1.75 us (2%)
    pallas_call x2, Pallas kernels, exchange(): pl.pallas_call(functools.partial(exchange_kernel, narrow, count), out_sha...  36.8 us
    pallas_call x1, Pallas kernels, on_device(): pl.pallas_call(levels_kernel, out_shape=jax.ShapeDtypeStruct((PARTS, E, W...  36.8 us
    unnamed x9, local copies, waits for them, and re-layouts  4.18 us
    pallas_call x1, Pallas kernels, on_device(): pl.pallas_call(pack_kernel, out_shape=jax.ShapeDtypeStruct((PARTS, E, W),...  3.19 us
    pallas_call x1, Pallas kernels, on_device(): pl.pallas_call(unpack_kernel, out_shape=jax.ShapeDtypeStruct((2, lines, W...  3.13 us

profile of v1, /device:TPU:1, one launch (start us, length us, event | category | flops | bytes accessed | tf_op | source)
XLA Modules:
  0.0 87.6 jit_solution(13932140634495646283)
XLA Ops:
  0.0 0.0 copy-start
  0.0 1.9 %copy.22 = f32[1,2,512,128]{3,2,1,0:T(8,128)} copy(f32[1,2,512,128]{3,1,2,0:T(2,128)} %bitcast.29) | data formatting | bytes 1048576
  1.9 0.0 copy-start.1
  1.9 3.2 %shard_map.82.refs_0_ = bf16[128,8,128]{2,1,0:T(8,128)(2,1)} custom-call(f32[2,512,128]{2,1,0:T(8,128)} %bitcast.24, s32[512,128]{1,0:T(8,128)} %bitcast.30), custom_call_target="tpu_custom_call" | custom-call | tf_op jit(solution)/shard_map/pallas_call | solution.py:314
  5.1 0.0 copy-done
  5.1 0.0 copy-start.2
  5.1 0.3 reshape.50
  5.4 0.2 copy.10
  5.6 0.1 reshape.51
  5.7 0.1 copy.11
  5.9 0.8 pad_maximum_fusion.refs_1_
  6.7 21.5 %shard_map.83 = (bf16[128,8,128]{2,1,0:T(8,128)(2,1)}, bf16[128,1,128]{2,1,0:T(2,128)(2,1)}) custom-call(bf16[128,8,128]{2,1,0:T(8,128)(2,1)} %shard_map.82.refs_0_, bf16[128,1,128]{2,1,0:T(2,128)(2,1)} %pad_maximum_fusion.refs_1_), custom_call_target="tpu_custom_call" | custom-call | tf_op jit(solution)/shard_map/pallas_call | solution.py:129
  28.2 0.0 copy-done.1
  28.2 0.1 broadcast_multiply_fusion
  28.4 0.8 copy.14.eval_map_ref
  29.2 0.1 copy.13
  29.3 0.0 copy-done.2
  29.3 0.8 broadcast_multiply_fusion.1
  30.1 36.8 %shard_map.84.refs_0_ = bf16[128,8,128]{2,1,0:T(8,128)(2,1)} custom-call(bf16[128,8,128]{2,1,0:T(8,128)(2,1)} %get-tuple-element.7.leaf_ref, bf16[128,1,128]{2,1,0:T(2,128)(2,1)} %get-tuple-element.8.speed_ref, bf16[128,1024]{1,0:T(8,128)(2,1)} %bitcast.25, bf16[10,2,2,128,128]{4,3,2,1,0:T(8,128)(2,1)} %mixing_ref.1, bf16[1024,128]{1,0:T(8,128)(2,1)} %copy.14.eval_map_ref, ...), custom_call_target="tpu_custom_call" | custom-call | tf_op jit(solution)/shard_map/pallas_call | solution.py:321
  66.9 15.3 %shard_map.85.field_ref = bf16[128,8,128]{2,1,0:T(8,128)(2,1)} custom-call(bf16[128,8,128]{2,1,0:T(8,128)(2,1)} %shard_map.84.refs_0_), custom_call_target="tpu_custom_call" | custom-call | tf_op jit(solution)/shard_map/pallas_call | solution.py:129
  82.2 3.1 %shard_map.86 = f32[2,512,128]{2,1,0:T(8,128)} custom-call(bf16[128,8,128]{2,1,0:T(8,128)(2,1)} %shard_map.85.field_ref, s32[512,128]{1,0:T(8,128)} %bitcast.31), custom_call_target="tpu_custom_call" | custom-call | tf_op jit(solution)/shard_map/pallas_call | solution.py:334
  85.4 2.2 %copy.21 = f32[1,2,512,128]{3,1,2,0:T(2,128)} copy(f32[1,2,512,128]{3,2,1,0:T(8,128)} %bitcast.23) | data formatting | bytes 1048576
  (2 shorter events, 0.1 us)
Async XLA Ops:
  0.0 5.1 %copy-start = (bf16[8192]{0:T(1024)(128)(2,1)S(1)}, bf16[8192]{0:T(1024)(128)(2,1)}, u32[]{:S(2)}) copy-start(bf16[8192]{0:T(1024)(128)(2,1)} %param.10) | copy-start | bytes 49156
  1.9 26.3 %copy-start.1 = (bf16[128,16]{0,1:T(8,128)(2,1)S(1)}, bf16[128,16]{0,1:T(8,128)(2,1)}, u32[]{:S(2)}) copy-start(bf16[128,16]{0,1:T(8,128)(2,1)} %param.13) | copy-start | bytes 12292
  5.1 24.2 %copy-start.2 = (bf16[16,128]{1,0:T(8,128)(2,1)S(1)}, bf16[16,128]{1,0:T(8,128)(2,1)}, u32[]{:S(2)}) copy-start(bf16[16,128]{1,0:T(8,128)(2,1)} %param.11) | copy-start | bytes 12292

commit v2 on v1

v2 whole, which is shorter than its diff:
```python
import functools
import math

import jax
import jax.numpy as jnp
import numpy as np
from jax import lax
from jax.experimental import pallas as pl
from jax.experimental.pallas import tpu as pltpu
from jax.sharding import PartitionSpec as P

MESH = pl.DeviceIdType.MESH
LEVELS = 10
PARTS = 128
E = 8
B = 8
W = 128


def half_sine_terms(count):
    w = 0.125 * (1 + np.cos(np.pi * (np.arange(64) + 0.5) / 64))
    u = np.sqrt(w)
    target = math.sqrt(2) * np.sin(np.pi * u) / u
    return np.polynomial.polynomial.polyfit(w, target, count - 1)


def phase_map():
    rank = W // 2
    nodes = np.cos(np.float32(math.pi) * (np.arange(rank, dtype=np.float32) + np.float32(0.5)) / np.float32(rank))
    rest = np.tile(nodes.astype(np.float64) * 0.5, 2)
    pieces = []
    for _ in range(3):
        pieces.append(rest.astype(jnp.bfloat16).astype(np.float64))
        rest = rest - pieces[-1]
    out = np.zeros((2, E, 2, B, B, W), np.float64)
    for b in range(B):
        out[0, :, 0, b, b, :] = pieces[0]
        out[0, :, 1, b, b, :] = pieces[1]
        out[1, :, :, b, b, :] = pieces[2]
    return out.reshape(2 * W, B * W).astype(jnp.bfloat16)


def low_half(shape):
    return lax.broadcasted_iota(jnp.int32, shape, len(shape) - 1) % W < W // 2


def half_turn(x):
    return pltpu.roll(x, W // 2, x.ndim - 1)


def slot_of(order):
    lane = lax.broadcasted_iota(jnp.int32, order.shape, 1)
    return (lane // 8) * 8 + order


def pack_rows(charges_ref, order_ref, out_ref):
    rows = 64
    half = PARTS // 2

    def body(step, _):
        at = pl.ds(pl.multiple_of(step * rows, rows), rows)
        index = slot_of(order_ref[at])
        first = charges_ref[pl.ds(pl.multiple_of(step * 2 * rows, 2 * rows), rows, stride=2)]
        second = charges_ref[pl.ds(step * 2 * rows + 1, rows, stride=2)]
        first = jnp.take_along_axis(first, index, axis=1, mode="promise_in_bounds")
        second = jnp.take_along_axis(second, index, axis=1, mode="promise_in_bounds")
        low = low_half(first.shape)
        even = jnp.where(low, first, half_turn(second)).astype(jnp.bfloat16)
        odd = jnp.where(low, half_turn(first), second).astype(jnp.bfloat16)
        out_ref[pl.ds(step * (rows // E), rows // E)] = even.reshape(rows // E, E, W)
        out_ref[pl.ds(half + step * (rows // E), rows // E)] = odd.reshape(rows // E, E, W)
        return 0

    lax.fori_loop(0, half * E // rows, body, 0)


def unpack_rows(field_ref, order_ref, out_ref):
    rows = 64
    half = PARTS // 2

    def body(step, _):
        at = pl.ds(pl.multiple_of(step * rows, rows), rows)
        index = slot_of(order_ref[at])
        even = field_ref[pl.ds(step * (rows // E), rows // E)].astype(jnp.float32).reshape(rows, W)
        odd = field_ref[pl.ds(half + step * (rows // E), rows // E)].astype(jnp.float32).reshape(rows, W)
        low = low_half(even.shape)
        first = jnp.where(low, even, half_turn(odd))
        second = jnp.where(low, half_turn(even), odd)
        first = jnp.take_along_axis(first, index, axis=1, mode="promise_in_bounds")
        second = jnp.take_along_axis(second, index, axis=1, mode="promise_in_bounds")
        out_ref[pl.ds(pl.multiple_of(step * 2 * rows, 2 * rows), rows, stride=2)] = first
        out_ref[pl.ds(step * 2 * rows + 1, rows, stride=2)] = second
        return 0

    lax.fori_loop(0, half * E // rows, body, 0)


def place(index, narrow):
    return (index // narrow, index % narrow)


def build_maps(leaf_ref, eval_ref, leaf_map_ref, eval_map_ref):
    leaf_map_ref[...] = jnp.zeros(leaf_map_ref.shape, jnp.bfloat16)
    for c in range(2):
        for b in range(B):
            rows = pl.ds(c * 64 + b * 8, 8)
            leaf_map_ref[rows, pl.ds(b * W, W)] = leaf_ref[pl.ds(c * 8, 8)]
    row = lax.broadcasted_iota(jnp.int32, (16, W), 0)
    lane = lax.broadcasted_iota(jnp.int32, (16, W), 1)
    slot = (lane // 64) * 8 + lane % 8 == row
    for b in range(B):
        pick = jnp.where(slot & (lane % 64 // 8 == b), 1.0, 0.0).astype(jnp.bfloat16)
        block = lax.dot_general(
            eval_ref[...], pick, (((0,), (0,)), ((), ())), preferred_element_type=jnp.float32
        )
        eval_map_ref[pl.ds(b * W, W)] = block.astype(jnp.bfloat16)


def rotate(pre, turn):
    low = low_half(turn.shape)
    other = half_turn(turn)
    cosine = jnp.where(low, turn, other)
    sine = jnp.where(low, -other, turn)
    return pre * cosine + half_turn(pre) * sine


def level_map(mixing_ref, level):
    return jnp.concatenate(
        [jnp.concatenate([mixing_ref[level, j, i] for i in range(2)], axis=0) for j in range(2)], axis=1
    )


def mix(near, far, maps):
    pre = jnp.dot(jnp.concatenate([near, far], axis=1), maps, preferred_element_type=jnp.float32)
    return [pre[:, :W], pre[:, W:]]


def pair_up(even, odd):
    rows = even.shape[0]
    both = jnp.concatenate([even.reshape(rows // E, E, W), odd.reshape(rows // E, E, W)], axis=1)
    return both.reshape(2 * rows, W)


TURN_ND, FIRST_ND, LATER_PAIRS, LAST_ND = 8, 32, 2, 16
PAIRS = B // 2
ROWS = PARTS * E
EARLY = {0: 0, 1: 1, LEVELS - 1: 2}


def make_turns(own_half, speed_ref, phase_ref, turn_p, turn_q):
    terms = half_sine_terms(5)
    nd = TURN_ND
    rows = nd * E

    def body(step, _):
        at = pl.ds(pl.multiple_of(step * nd, nd), nd)
        speeds = jnp.broadcast_to(speed_ref[at], (nd, E, W)).reshape(rows, W)
        lane = lax.broadcasted_iota(jnp.int32, (rows, W), 1)
        row = lax.broadcasted_iota(jnp.int32, (rows, W), 0)
        mine = (lane // 16 == row % E) & (lane // B % 2 == own_half)
        own = jnp.where(mine, speeds, 0.0)
        operand = jnp.concatenate([own + pltpu.roll(own, B, 1), own], axis=1).astype(jnp.bfloat16)
        counts = jnp.dot(operand, phase_ref[...], preferred_element_type=jnp.float32)
        low = low_half((rows, W))
        start = jnp.where(low, 1.0, 0.0)
        quarter = jnp.where(low, 0.0, 0.25)
        rows_at = pl.ds(pl.multiple_of(step * rows, rows), rows)
        wide_at = pl.ds(pl.multiple_of(step * rows * 2, rows * 2), rows * 2)
        for pair in range(PAIRS):
            now, before, twice = [], [start, start], []
            for b in (2 * pair, 2 * pair + 1):
                u = counts[:, b * W : (b + 1) * W] - quarter
                u = u - jnp.round(u)
                w = u * u
                p = w * jnp.float32(terms[4]) + jnp.float32(terms[3])
                for k in (2, 1, 0):
                    p = p * w + jnp.float32(terms[k])
                s = u * p
                t = 1.0 - s * s
                now.append(t)
                c = jnp.where(low, t, half_turn(t))
                twice.append(c + c)
            for level in range(LEVELS):
                if level in EARLY:
                    for i in range(2):
                        turn_p[EARLY[level], 2 * pair + i, rows_at] = now[i].astype(jnp.bfloat16)
                else:
                    turn_q[level - 2, pair, wide_at] = pair_up(now[0], now[1]).astype(jnp.bfloat16)
                if level < LEVELS - 1:
                    now, before = [twice[i] * now[i] - before[i] for i in range(2)], now
        return 0

    lax.fori_loop(0, PARTS // nd, body, 0)


def first_levels(leaf_ref, leaf_map_ref, mixing_ref, turn_p, turn_q, state):
    nd = FIRST_ND
    rows = nd * E

    def body(step, _):
        at = pl.ds(pl.multiple_of(step * nd, nd), nd)
        rows_at = pl.ds(pl.multiple_of(step * rows, rows), rows)
        wide_at = pl.ds(pl.multiple_of(step * rows * 2, rows * 2), rows * 2)
        leaf = leaf_ref[at].reshape(rows, W)
        boxes = [None] * B
        maps = level_map(mixing_ref, 0)
        for pair in range(PAIRS):
            lanes = pl.ds(pair * 2 * W, 2 * W)
            spread = jnp.dot(leaf, leaf_map_ref[:, lanes], preferred_element_type=jnp.float32)
            pre = jnp.dot(spread.astype(jnp.bfloat16), maps, preferred_element_type=jnp.float32)
            for i in range(2):
                b = 2 * pair + i
                boxes[b] = rotate(pre[:, i * W : (i + 1) * W].astype(jnp.bfloat16), turn_p[0, b, rows_at])
        maps = level_map(mixing_ref, 1)
        for b in (0, 1, 4, 5):
            for i, pre in enumerate(mix(boxes[b], boxes[b + 2], maps)):
                boxes[b + 2 * i] = rotate(pre.astype(jnp.bfloat16), turn_p[1, b + 2 * i, rows_at])
        maps = level_map(mixing_ref, 2)
        for pair in range(2):
            pres = [mix(boxes[2 * pair + i], boxes[2 * pair + i + 4], maps) for i in range(2)]
            for i in range(2):
                pre = pair_up(pres[0][i], pres[1][i]).astype(jnp.bfloat16)
                state[pair + 2 * i, wide_at] = rotate(pre, turn_q[0, pair + 2 * i, wide_at])
        return 0

    lax.fori_loop(0, PARTS // nd, body, 0)


def later_level(level, mixing_ref, turn_q, source, target):
    stride = 2 * E << (level - 3)
    starts = range(0, 2 * ROWS, 2 * stride)

    def body(step, _):
        maps = level_map(mixing_ref, level)
        for i in range(LATER_PAIRS):
            pair = step * LATER_PAIRS + i
            near = jnp.concatenate([source[pair, pl.ds(at, stride)] for at in starts], axis=0)
            far = jnp.concatenate([source[pair, pl.ds(at + stride, stride)] for at in starts], axis=0)
            for side, pre in enumerate(mix(near, far, maps)):
                for n, at in enumerate(starts):
                    rows_at = pl.ds(at + side * stride, stride)
                    part = pre[n * stride : (n + 1) * stride].astype(jnp.bfloat16)
                    target[pair, rows_at] = rotate(part, turn_q[level - 2, pair, rows_at])
        return 0

    lax.fori_loop(0, PAIRS // LATER_PAIRS, body, 0)


def last_level(me, send, mixing_ref, eval_map_ref, turn_p, state, out_ref):
    level = LEVELS - 1
    nd = LAST_ND
    rows = nd * E
    steps = PARTS // 2 // nd

    def body(count, _):
        step = (count + me // nd) % steps
        maps = level_map(mixing_ref, level)
        boxes = [[], []]
        wide = [pl.ds(pl.multiple_of(step * 2 * rows + side * ROWS, 2 * rows), 2 * rows) for side in range(2)]
        for pair in range(PAIRS):
            for side, pre in enumerate(mix(state[pair, wide[0]], state[pair, wide[1]], maps)):
                own = pre.reshape(nd, 2, E, W)
                rows_at = pl.ds(pl.multiple_of(step * rows + side * (ROWS // 2), rows), rows)
                for i in range(2):
                    box = own[:, i].reshape(rows, W).astype(jnp.bfloat16)
                    boxes[side].append(rotate(box, turn_p[EARLY[level], 2 * pair + i, rows_at]))
        for side in range(2):
            values = jnp.dot(
                jnp.concatenate(boxes[side], axis=1), eval_map_ref[...], preferred_element_type=jnp.float32
            )
            at = pl.ds(step * nd + side * (PARTS // 2), nd)
            out_ref[at] = values.astype(jnp.bfloat16).reshape(nd, E, W)

        def one(i, _):
            for side in range(2):
                send(step * nd + side * (PARTS // 2) + ((i + me) % nd))
            return 0

        lax.fori_loop(0, nd, one, 0)
        return 0

    lax.fori_loop(0, steps, body, 0)


def kernel(
    narrow, charges_hbm, order_hbm, speed_hbm, leaf_hbm, mixing_hbm, eval_hbm, target_hbm, phase_hbm, out_hbm,
    charges, order, speed, leaf_weight, mixing, eval_weight, target, phase,
    speed_rows, speeds, packed, leaf, result, field, out, leaf_map, eval_map, state, spare, turn_p, turn_q,
    load_sems, sends, recvs, store_sem,
):
    me = lax.axis_index("wide") * narrow + lax.axis_index("narrow")
    barrier = pltpu.get_barrier_semaphore()

    def greet(k, _):
        pl.semaphore_signal(barrier, inc=1, device_id=place(me ^ k, narrow), device_id_type=MESH)
        return 0

    lax.fori_loop(1, PARTS, greet, 0)
    pairs = (
        (speed_hbm, speed), (order_hbm, order), (charges_hbm, charges), (leaf_hbm, leaf_weight),
        (eval_hbm, eval_weight), (phase_hbm, phase), (mixing_hbm, mixing), (target_hbm, target),
    )
    loads = [pltpu.make_async_copy(a, b, load_sems.at[i]) for i, (a, b) in enumerate(pairs)]
    for load in loads:
        load.start()
    half = PARTS // 2
    loads[0].wait()
    speed_rows[...] = speed[...].astype(jnp.float32).reshape(half, 1, W)
    loads[1].wait()
    loads[2].wait()
    pack_rows(charges, order, packed)
    loads[3].wait()
    loads[4].wait()
    build_maps(leaf_weight, eval_weight, leaf_map, eval_map)
    pl.semaphore_wait(barrier, PARTS - 1)

    def remote(source, target, i, to):
        return pltpu.make_async_remote_copy(
            source, target.at[me], sends.at[i], recvs.at[i], device_id=place(to, narrow), device_id_type=MESH
        )

    def send_speed(k, _):
        to = me ^ k
        remote(speed_rows.at[to % half], speeds, 0, to).start()
        return 0

    def send_leaf(k, _):
        to = me ^ k
        remote(packed.at[to], leaf, 1, to).start()
        return 0

    lax.fori_loop(1, PARTS, send_speed, 0)
    lax.fori_loop(1, PARTS, send_leaf, 0)
    speeds[me] = speed_rows[me % half]
    leaf[me] = packed[me]
    others = pl.ds(0, PARTS - 1)

    def wait(ref, sem):
        pltpu.make_async_copy(ref.at[others], ref.at[others], sem).wait()

    loads[5].wait()
    wait(speeds, recvs.at[0])
    make_turns(me // half, speeds, phase, turn_p, turn_q)
    loads[6].wait()
    wait(leaf, recvs.at[1])
    first_levels(leaf, leaf_map, mixing, turn_p, turn_q, state)
    now, later = state, spare
    for level in range(3, LEVELS - 1):
        later_level(level, mixing, turn_q, now, later)
        now, later = later, now

    def send_result(to):
        @pl.when(to != me)
        def _():
            remote(result.at[to], field, 2, to).start()

    last_level(me, send_result, mixing, eval_map, turn_p, now, result)
    field[me] = result[me]
    loads[7].wait()
    wait(field, recvs.at[2])
    unpack_rows(field, target, out)
    store = pltpu.make_async_copy(out, out_hbm, store_sem)
    store.start()
    wait(speeds, sends.at[0])
    wait(packed, sends.at[1])
    wait(result, sends.at[2])
    store.wait()


def on_device(narrow, charges, source_order, velocity, leaf_weight, mixing, eval_weight, target_order):
    lines = charges.shape[1] // W
    half = PARTS // 2
    args = (
        charges.reshape(2, lines, W).transpose(1, 0, 2).reshape(2 * lines, W),
        source_order.reshape(lines, W),
        velocity.reshape(half, W),
        leaf_weight,
        mixing,
        eval_weight.T,
        target_order.reshape(lines, W),
        jnp.asarray(phase_map()),
    )
    chunk = pltpu.VMEM((PARTS, E, W), jnp.bfloat16)
    states = pltpu.VMEM((PAIRS, 2 * ROWS, W), jnp.bfloat16)
    rows = pltpu.VMEM((2 * lines, W), jnp.float32)
    out = pl.pallas_call(
        functools.partial(kernel, narrow),
        out_shape=jax.ShapeDtypeStruct((2 * lines, W), jnp.float32),
        in_specs=[pl.BlockSpec(memory_space=pltpu.HBM)] * len(args),
        out_specs=pl.BlockSpec(memory_space=pltpu.HBM),
        scratch_shapes=[pltpu.VMEM(a.shape, a.dtype) for a in args]
        + [
            pltpu.VMEM((half, 1, W), jnp.float32),
            pltpu.VMEM((PARTS, 1, W), jnp.float32),
            chunk,
            chunk,
            chunk,
            chunk,
            rows,
            pltpu.VMEM((W, B * W), jnp.bfloat16),
            pltpu.VMEM((B * W, W), jnp.bfloat16),
            states,
            states,
            pltpu.VMEM((len(EARLY), B, ROWS, W), jnp.bfloat16),
            pltpu.VMEM((LEVELS - len(EARLY), PAIRS, 2 * ROWS, W), jnp.bfloat16),
            pltpu.SemaphoreType.DMA((len(args),)),
            pltpu.SemaphoreType.DMA((3,)),
            pltpu.SemaphoreType.DMA((3,)),
            pltpu.SemaphoreType.DMA,
        ],
        compiler_params=pltpu.CompilerParams(
            has_side_effects=True, collective_id=0, vmem_limit_bytes=62 * 2**20
        ),
    )(*args)
    return out.reshape(lines, 2, W).transpose(1, 0, 2).reshape(2, lines * W)


def solution(mesh):
    both = ("wide", "narrow")
    return jax.shard_map(
        functools.partial(on_device, mesh.shape["narrow"]),
        mesh=mesh,
        in_specs=(P(None, both), P(both), P(both), P(), P(), P(), P(both)),
        out_specs=P(None, both),
        check_vma=False,
    )
```

time: 87.9 us -> 57.9 us (0.66)
  Pallas kernels: 79.9 us -> 55.8 us
  local copies, waits for them, and re-layouts: 5.86 us -> 1.87 us
  other arithmetic: 1.75 us -> 0 us
    pallas_call x5 -> x1, Pallas kernels: 79.9 us -> 55.8 us  [on_device(): pl.pallas_call(functools.partial(kernel, narrow), out_shape=jax.ShapeDtyp...]
    unnamed x9 -> x1, local copies, waits for them, and re-layouts: 4.18 us -> 1.87 us
    mul x2 -> x0, other arithmetic: 0.93 us -> none  [the longest x1 0.84 us: on_device(): leaf_map = leaf_weight.reshape(2, 1, 8, 1, W) * eye.reshape(1, B, 1, B, 1)]
where the time goes in v2:
time: 57.9 us; the launch traced here: 57.7 us
  Pallas kernels  55.8 us (96%)
  local copies, waits for them, and re-layouts  1.87 us (3%)
    pallas_call x1, Pallas kernels, on_device(): pl.pallas_call(functools.partial(kernel, narrow), out_shape=jax.ShapeDtyp...  55.8 us
    unnamed x1, local copies, waits for them, and re-layouts  1.87 us

profile of v2, /device:TPU:1, one launch (start us, length us, event | category | flops | bytes accessed | tf_op | source)
XLA Modules:
  0.0 57.7 jit_solution(8693770988973454088)
XLA Ops:
  0.0 55.8 %shard_map.82 = f32[1024,128]{1,0:T(8,128)} custom-call(f32[1024,128]{1,0:T(8,128)} %bitcast.15, s32[512,128]{1,0:T(8,128)} %bitcast.16, bf16[64,128]{1,0:T(8,128)(2,1)} %bitcast.18, bf16[16,128]{1,0:T(8,128)(2,1)} %leaf_hbm.1, bf16[10,2,2,128,128]{4,3,2,1,0:T(8,128)(2,1)} %mixing_hbm.1, bf16[16,128]{1,0:T(8,128)(2,1)} %bitcast.19, s32[512,128]{1,0:T(8,128)} %bitcast.17, ...), custom_call_target="tpu_custom_call" | custom-call | tf_op jit(solution)/shard_map/pallas_call | solution.py:386
  55.8 1.9 %copy.12 = f32[2,65536]{1,0:T(2,128)} copy(f32[2,65536]{1,0:T(2,128)} %bitcast.14) | data formatting | bytes 1048576

commit v3 on v2

--- a/solution.py
+++ b/solution.py
@@ -116,11 +116,7 @@
         eval_map_ref[pl.ds(b * W, W)] = block.astype(jnp.bfloat16)
 
 
-def rotate(pre, turn):
-    low = low_half(turn.shape)
-    other = half_turn(turn)
-    cosine = jnp.where(low, turn, other)
-    sine = jnp.where(low, -other, turn)
+def rotate(pre, cosine, sine):
     return pre * cosine + half_turn(pre) * sine
 
 
@@ -141,14 +137,14 @@
     return both.reshape(2 * rows, W)
 
 
-TURN_ND, FIRST_ND, LATER_PAIRS, LAST_ND = 8, 32, 2, 16
+TURN_ND, FIRST_ND, LATER_PAIRS, LAST_ND = 8, 64, 2, 16
 PAIRS = B // 2
 ROWS = PARTS * E
 EARLY = {0: 0, 1: 1, LEVELS - 1: 2}
 
 
-def make_turns(own_half, speed_ref, phase_ref, turn_p, turn_q):
-    terms = half_sine_terms(5)
+def make_turns(own_half, speed_ref, phase_ref, cos_p, sin_p, cos_q, sin_q):
+    terms = half_sine_terms(4)
     nd = TURN_ND
     rows = nd * E
 
@@ -162,38 +158,49 @@
         operand = jnp.concatenate([own + pltpu.roll(own, B, 1), own], axis=1).astype(jnp.bfloat16)
         counts = jnp.dot(operand, phase_ref[...], preferred_element_type=jnp.float32)
         low = low_half((rows, W))
-        start = jnp.where(low, 1.0, 0.0)
         quarter = jnp.where(low, 0.0, 0.25)
         rows_at = pl.ds(pl.multiple_of(step * rows, rows), rows)
         wide_at = pl.ds(pl.multiple_of(step * rows * 2, rows * 2), rows * 2)
         for pair in range(PAIRS):
-            now, before, twice = [], [start, start], []
+            cosine, sine, twice = [], [], []
             for b in (2 * pair, 2 * pair + 1):
                 u = counts[:, b * W : (b + 1) * W] - quarter
                 u = u - jnp.round(u)
                 w = u * u
-                p = w * jnp.float32(terms[4]) + jnp.float32(terms[3])
-                for k in (2, 1, 0):
+                p = w * jnp.float32(terms[3]) + jnp.float32(terms[2])
+                for k in (1, 0):
                     p = p * w + jnp.float32(terms[k])
                 s = u * p
                 t = 1.0 - s * s
-                now.append(t)
-                c = jnp.where(low, t, half_turn(t))
-                twice.append(c + c)
+                other = half_turn(t)
+                cosine.append(jnp.where(low, t, other))
+                sine.append(jnp.where(low, -other, t))
+                twice.append(cosine[-1] + cosine[-1])
+            last = None
             for level in range(LEVELS):
-                if level in EARLY:
-                    for i in range(2):
-                        turn_p[EARLY[level], 2 * pair + i, rows_at] = now[i].astype(jnp.bfloat16)
+                for now, early, late in ((cosine, cos_p, cos_q), (sine, sin_p, sin_q)):
+                    if level in EARLY:
+                        for i in range(2):
+                            early[EARLY[level], 2 * pair + i, rows_at] = now[i].astype(jnp.bfloat16)
+                    else:
+                        late[level - 2, pair, wide_at] = pair_up(now[0], now[1]).astype(jnp.bfloat16)
+                if level == LEVELS - 1:
+                    break
+                if last is None:
+                    after = [twice[i] * cosine[i] - 1.0 for i in range(2)], [twice[i] * sine[i] for i in range(2)]
                 else:
-                    turn_q[level - 2, pair, wide_at] = pair_up(now[0], now[1]).astype(jnp.bfloat16)
-                if level < LEVELS - 1:
-                    now, before = [twice[i] * now[i] - before[i] for i in range(2)], now
+                    after = [
+                        [twice[i] * now[i] - before[i] for i in range(2)]
+                        for now, before in ((cosine, last[0]), (sine, last[1]))
+                    ]
+                last = cosine, sine
+                cosine, sine = after
         return 0
 
     lax.fori_loop(0, PARTS // nd, body, 0)
 
 
-def first_levels(leaf_ref, leaf_map_ref, mixing_ref, turn_p, turn_q, state):
+def first_levels(leaf_ref, leaf_map_ref, mixing_ref, cos_p, sin_p, cos_q, sin_q, state):
     nd = FIRST_ND
     rows = nd * E
 
@@ -210,23 +217,25 @@
             pre = jnp.dot(spread.astype(jnp.bfloat16), maps, preferred_element_type=jnp.float32)
             for i in range(2):
                 b = 2 * pair + i
-                boxes[b] = rotate(pre[:, i * W : (i + 1) * W].astype(jnp.bfloat16), turn_p[0, b, rows_at])
+                boxes[b] = rotate(pre[:, i * W : (i + 1) * W].astype(jnp.bfloat16), cos_p[0, b, rows_at], sin_p[0, b, rows_at])
         maps = level_map(mixing_ref, 1)
         for b in (0, 1, 4, 5):
             for i, pre in enumerate(mix(boxes[b], boxes[b + 2], maps)):
-                boxes[b + 2 * i] = rotate(pre.astype(jnp.bfloat16), turn_p[1, b + 2 * i, rows_at])
+                box = b + 2 * i
+                boxes[box] = rotate(pre.astype(jnp.bfloat16), cos_p[1, box, rows_at], sin_p[1, box, rows_at])
         maps = level_map(mixing_ref, 2)
         for pair in range(2):
             pres = [mix(boxes[2 * pair + i], boxes[2 * pair + i + 4], maps) for i in range(2)]
             for i in range(2):
                 pre = pair_up(pres[0][i], pres[1][i]).astype(jnp.bfloat16)
-                state[pair + 2 * i, wide_at] = rotate(pre, turn_q[0, pair + 2 * i, wide_at])
+                unit = pair + 2 * i
+                state[unit, wide_at] = rotate(pre, cos_q[0, unit, wide_at], sin_q[0, unit, wide_at])
         return 0
 
     lax.fori_loop(0, PARTS // nd, body, 0)
 
 
-def later_level(level, mixing_ref, turn_q, source, target):
+def later_level(level, mixing_ref, cos_q, sin_q, source, target):
     stride = 2 * E << (level - 3)
     starts = range(0, 2 * ROWS, 2 * stride)
 
@@ -240,13 +249,15 @@
                 for n, at in enumerate(starts):
                     rows_at = pl.ds(at + side * stride, stride)
                     part = pre[n * stride : (n + 1) * stride].astype(jnp.bfloat16)
-                    target[pair, rows_at] = rotate(part, turn_q[level - 2, pair, rows_at])
+                    target[pair, rows_at] = rotate(
+                        part, cos_q[level - 2, pair, rows_at], sin_q[level - 2, pair, rows_at]
+                    )
         return 0
 
     lax.fori_loop(0, PAIRS // LATER_PAIRS, body, 0)
 
 
-def last_level(me, send, mixing_ref, eval_map_ref, turn_p, state, out_ref):
+def last_level(me, send, mixing_ref, eval_map_ref, cos_p, sin_p, state, out_ref):
     level = LEVELS - 1
     nd = LAST_ND
     rows = nd * E
@@ -263,7 +274,8 @@
                 rows_at = pl.ds(pl.multiple_of(step * rows + side * (ROWS // 2), rows), rows)
                 for i in range(2):
                     box = own[:, i].reshape(rows, W).astype(jnp.bfloat16)
-                    boxes[side].append(rotate(box, turn_p[EARLY[level], 2 * pair + i, rows_at]))
+                    at = EARLY[level], 2 * pair + i, rows_at
+                    boxes[side].append(rotate(box, cos_p[at], sin_p[at]))
         for side in range(2):
             values = jnp.dot(
                 jnp.concatenate(boxes[side], axis=1), eval_map_ref[...], preferred_element_type=jnp.float32
@@ -285,7 +297,7 @@
 def kernel(
     narrow, charges_hbm, order_hbm, speed_hbm, leaf_hbm, mixing_hbm, eval_hbm, target_hbm, phase_hbm, out_hbm,
     charges, order, speed, leaf_weight, mixing, eval_weight, target, phase,
-    speed_rows, speeds, packed, leaf, result, field, out, leaf_map, eval_map, state, spare, turn_p, turn_q,
+    speed_rows, speeds, packed, leaf, result, field, out, leaf_map, eval_map, state, spare, cos_p, sin_p, cos_q, sin_q,
     load_sems, sends, recvs, store_sem,
 ):
     me = lax.axis_index("wide") * narrow + lax.axis_index("narrow")
@@ -340,13 +352,13 @@
 
     loads[5].wait()
     wait(speeds, recvs.at[0])
-    make_turns(me // half, speeds, phase, turn_p, turn_q)
+    make_turns(me // half, speeds, phase, cos_p, sin_p, cos_q, sin_q)
     loads[6].wait()
     wait(leaf, recvs.at[1])
-    first_levels(leaf, leaf_map, mixing, turn_p, turn_q, state)
+    first_levels(leaf, leaf_map, mixing, cos_p, sin_p, cos_q, sin_q, state)
     now, later = state, spare
     for level in range(3, LEVELS - 1):
-        later_level(level, mixing, turn_q, now, later)
+        later_level(level, mixing, cos_q, sin_q, now, later)
         now, later = later, now
 
     def send_result(to):
@@ -354,7 +366,7 @@
         def _():
             remote(result.at[to], field, 2, to).start()
 
-    last_level(me, send_result, mixing, eval_map, turn_p, now, result)
+    last_level(me, send_result, mixing, eval_map, cos_p, sin_p, now, result)
     field[me] = result[me]
     loads[7].wait()
     wait(field, recvs.at[2])
@@ -402,6 +414,8 @@
             states,
             states,
             pltpu.VMEM((len(EARLY), B, ROWS, W), jnp.bfloat16),
+            pltpu.VMEM((len(EARLY), B, ROWS, W), jnp.bfloat16),
+            pltpu.VMEM((LEVELS - len(EARLY), PAIRS, 2 * ROWS, W), jnp.bfloat16),
             pltpu.VMEM((LEVELS - len(EARLY), PAIRS, 2 * ROWS, W), jnp.bfloat16),
             pltpu.SemaphoreType.DMA((len(args),)),
             pltpu.SemaphoreType.DMA((3,)),

time: 57.9 us -> 55.1 us (0.952)
  Pallas kernels: 55.8 us -> 53.1 us
    pallas_call x1, Pallas kernels: 55.8 us -> 53.1 us  [on_device(): pl.pallas_call(functools.partial(kernel, narrow), out_shape=jax.ShapeDtyp...]
where the time goes in v3:
time: 55.1 us; the launch traced here: 54.9 us
  Pallas kernels  53.1 us (96%)
  local copies, waits for them, and re-layouts  1.87 us (3%)
    pallas_call x1, Pallas kernels, on_device(): pl.pallas_call(functools.partial(kernel, narrow), out_shape=jax.ShapeDtyp...  53.1 us
    unnamed x1, local copies, waits for them, and re-layouts  1.87 us

profile of v3, /device:TPU:1, one launch (start us, length us, event | category | flops | bytes accessed | tf_op | source)
XLA Modules:
  0.0 54.9 jit_solution(1149752572389153391)
XLA Ops:
  0.0 53.1 %shard_map.82 = f32[1024,128]{1,0:T(8,128)} custom-call(f32[1024,128]{1,0:T(8,128)} %bitcast.15, s32[512,128]{1,0:T(8,128)} %bitcast.16, bf16[64,128]{1,0:T(8,128)(2,1)} %bitcast.18, bf16[16,128]{1,0:T(8,128)(2,1)} %leaf_hbm.1, bf16[10,2,2,128,128]{4,3,2,1,0:T(8,128)(2,1)} %mixing_hbm.1, bf16[16,128]{1,0:T(8,128)(2,1)} %bitcast.19, s32[512,128]{1,0:T(8,128)} %bitcast.17, ...), custom_call_target="tpu_custom_call" | custom-call | tf_op jit(solution)/shard_map/pallas_call | solution.py:398
  53.1 1.9 %copy.12 = f32[2,65536]{1,0:T(2,128)} copy(f32[2,65536]{1,0:T(2,128)} %bitcast.14) | data formatting | bytes 1048576

commit v4 on v3

--- a/solution.py
+++ b/solution.py
@@ -74,25 +74,16 @@
     lax.fori_loop(0, half * E // rows, body, 0)
 
 
-def unpack_rows(field_ref, order_ref, out_ref):
-    rows = 64
-    half = PARTS // 2
-
-    def body(step, _):
-        at = pl.ds(pl.multiple_of(step * rows, rows), rows)
-        index = slot_of(order_ref[at])
-        even = field_ref[pl.ds(step * (rows // E), rows // E)].astype(jnp.float32).reshape(rows, W)
-        odd = field_ref[pl.ds(half + step * (rows // E), rows // E)].astype(jnp.float32).reshape(rows, W)
-        low = low_half(even.shape)
-        first = jnp.where(low, even, half_turn(odd))
-        second = jnp.where(low, half_turn(even), odd)
-        first = jnp.take_along_axis(first, index, axis=1, mode="promise_in_bounds")
-        second = jnp.take_along_axis(second, index, axis=1, mode="promise_in_bounds")
-        out_ref[pl.ds(pl.multiple_of(step * 2 * rows, 2 * rows), rows, stride=2)] = first
-        out_ref[pl.ds(step * 2 * rows + 1, rows, stride=2)] = second
-        return 0
-
-    lax.fori_loop(0, half * E // rows, body, 0)
+def unpack_kernel(field_ref, order_ref, out_ref):
+    rows = order_ref.shape[0]
+    index = slot_of(order_ref[...])
+    even = field_ref[0].astype(jnp.float32).reshape(rows, W)
+    odd = field_ref[1].astype(jnp.float32).reshape(rows, W)
+    low = low_half(even.shape)
+    first = jnp.where(low, even, half_turn(odd))
+    second = jnp.where(low, half_turn(even), odd)
+    out_ref[pl.ds(0, rows, stride=2)] = jnp.take_along_axis(first, index, axis=1, mode="promise_in_bounds")
+    out_ref[pl.ds(1, rows, stride=2)] = jnp.take_along_axis(second, index, axis=1, mode="promise_in_bounds")
 
 
 def place(index, narrow):
@@ -143,17 +134,19 @@
 EARLY = {0: 0, 1: 1, LEVELS - 1: 2}
 
 
-def make_turns(own_half, speed_ref, phase_ref, cos_p, sin_p, cos_q, sin_q):
-    terms = half_sine_terms(4)
+def make_turns(me, arrived, speed_ref, phase_ref, cos_p, sin_p, cos_q, sin_q):
+    terms = half_sine_terms(5)
     nd = TURN_ND
     rows = nd * E
 
-    def body(step, _):
+    def body(count, _):
+        arrived(count)
+        step = count ^ me // nd
         at = pl.ds(pl.multiple_of(step * nd, nd), nd)
         speeds = jnp.broadcast_to(speed_ref[at], (nd, E, W)).reshape(rows, W)
         lane = lax.broadcasted_iota(jnp.int32, (rows, W), 1)
         row = lax.broadcasted_iota(jnp.int32, (rows, W), 0)
-        mine = (lane // 16 == row % E) & (lane // B % 2 == own_half)
+        mine = (lane // 16 == row % E) & (lane // B % 2 == me // (PARTS // 2))
         own = jnp.where(mine, speeds, 0.0)
         operand = jnp.concatenate([own + pltpu.roll(own, B, 1), own], axis=1).astype(jnp.bfloat16)
         counts = jnp.dot(operand, phase_ref[...], preferred_element_type=jnp.float32)
@@ -167,8 +160,8 @@
                 u = counts[:, b * W : (b + 1) * W] - quarter
                 u = u - jnp.round(u)
                 w = u * u
-                p = w * jnp.float32(terms[3]) + jnp.float32(terms[2])
-                for k in (1, 0):
+                p = w * jnp.float32(terms[4]) + jnp.float32(terms[3])
+                for k in (2, 1, 0):
                     p = p * w + jnp.float32(terms[k])
                 s = u * p
                 t = 1.0 - s * s
@@ -295,10 +288,10 @@
 
 
 def kernel(
-    narrow, charges_hbm, order_hbm, speed_hbm, leaf_hbm, mixing_hbm, eval_hbm, target_hbm, phase_hbm, out_hbm,
-    charges, order, speed, leaf_weight, mixing, eval_weight, target, phase,
-    speed_rows, speeds, packed, leaf, result, field, out, leaf_map, eval_map, state, spare, cos_p, sin_p, cos_q, sin_q,
-    load_sems, sends, recvs, store_sem,
+    narrow, charges_hbm, order_hbm, speed_hbm, leaf_hbm, mixing_hbm, eval_hbm, phase_hbm, field,
+    charges, order, speed, leaf_weight, mixing, eval_weight, phase,
+    speed_rows, speeds, packed, leaf, result, leaf_map, eval_map, state, spare, cos_p, sin_p, cos_q, sin_q,
+    load_sems, sends, recvs, speed_recvs, own_sem,
 ):
     me = lax.axis_index("wide") * narrow + lax.axis_index("narrow")
     barrier = pltpu.get_barrier_semaphore()
@@ -310,7 +303,7 @@
     lax.fori_loop(1, PARTS, greet, 0)
     pairs = (
         (speed_hbm, speed), (order_hbm, order), (charges_hbm, charges), (leaf_hbm, leaf_weight),
-        (eval_hbm, eval_weight), (phase_hbm, phase), (mixing_hbm, mixing), (target_hbm, target),
+        (eval_hbm, eval_weight), (phase_hbm, phase), (mixing_hbm, mixing),
     )
     loads = [pltpu.make_async_copy(a, b, load_sems.at[i]) for i, (a, b) in enumerate(pairs)]
     for load in loads:
@@ -326,35 +319,43 @@
     build_maps(leaf_weight, eval_weight, leaf_map, eval_map)
     pl.semaphore_wait(barrier, PARTS - 1)
 
-    def remote(source, target, i, to):
+    def remote(source, target, i, to, recv):
         return pltpu.make_async_remote_copy(
-            source, target.at[me], sends.at[i], recvs.at[i], device_id=place(to, narrow), device_id_type=MESH
+            source, target.at[me], sends.at[i], recv, device_id=place(to, narrow), device_id_type=MESH
         )
 
     def send_speed(k, _):
         to = me ^ k
-        remote(speed_rows.at[to % half], speeds, 0, to).start()
+        remote(speed_rows.at[to % half], speeds, 0, to, speed_recvs.at[k // TURN_ND]).start()
         return 0
 
     def send_leaf(k, _):
         to = me ^ k
-        remote(packed.at[to], leaf, 1, to).start()
+        remote(packed.at[to], leaf, 1, to, recvs.at[0]).start()
         return 0
 
     lax.fori_loop(1, PARTS, send_speed, 0)
     lax.fori_loop(1, PARTS, send_leaf, 0)
     speeds[me] = speed_rows[me % half]
     leaf[me] = packed[me]
-    others = pl.ds(0, PARTS - 1)
-
-    def wait(ref, sem):
-        pltpu.make_async_copy(ref.at[others], ref.at[others], sem).wait()
+
+    def wait(ref, sem, count=PARTS - 1):
+        some = pl.ds(0, count)
+        pltpu.make_async_copy(ref.at[some], ref.at[some], sem).wait()
+
+    def arrived(count):
+        @pl.when(count == 0)
+        def _():
+            wait(speeds, speed_recvs.at[count], TURN_ND - 1)
+
+        @pl.when(count > 0)
+        def _():
+            wait(speeds, speed_recvs.at[count], TURN_ND)
 
     loads[5].wait()
-    wait(speeds, recvs.at[0])
-    make_turns(me // half, speeds, phase, cos_p, sin_p, cos_q, sin_q)
+    make_turns(me, arrived, speeds, phase, cos_p, sin_p, cos_q, sin_q)
     loads[6].wait()
-    wait(leaf, recvs.at[1])
+    wait(leaf, recvs.at[0])
     first_levels(leaf, leaf_map, mixing, cos_p, sin_p, cos_q, sin_q, state)
     now, later = state, spare
     for level in range(3, LEVELS - 1):
@@ -364,19 +365,16 @@
     def send_result(to):
         @pl.when(to != me)
         def _():
-            remote(result.at[to], field, 2, to).start()
+            remote(result.at[to], field, 2, to, recvs.at[1]).start()
 
     last_level(me, send_result, mixing, eval_map, cos_p, sin_p, now, result)
-    field[me] = result[me]
-    loads[7].wait()
-    wait(field, recvs.at[2])
-    unpack_rows(field, target, out)
-    store = pltpu.make_async_copy(out, out_hbm, store_sem)
-    store.start()
+    own = pltpu.make_async_copy(result.at[me], field.at[me], own_sem)
+    own.start()
     wait(speeds, sends.at[0])
     wait(packed, sends.at[1])
+    wait(result, recvs.at[1])
     wait(result, sends.at[2])
-    store.wait()
+    own.wait()
 
 
 def on_device(narrow, charges, source_order, velocity, leaf_weight, mixing, eval_weight, target_order):
@@ -389,15 +387,13 @@
         leaf_weight,
         mixing,
         eval_weight.T,
-        target_order.reshape(lines, W),
         jnp.asarray(phase_map()),
     )
     chunk = pltpu.VMEM((PARTS, E, W), jnp.bfloat16)
     states = pltpu.VMEM((PAIRS, 2 * ROWS, W), jnp.bfloat16)
-    rows = pltpu.VMEM((2 * lines, W), jnp.float32)
-    out = pl.pallas_call(
+    field = pl.pallas_call(
         functools.partial(kernel, narrow),
-        out_shape=jax.ShapeDtypeStruct((2 * lines, W), jnp.float32),
+        out_shape=jax.ShapeDtypeStruct((PARTS, E, W), jnp.bfloat16),
         in_specs=[pl.BlockSpec(memory_space=pltpu.HBM)] * len(args),
         out_specs=pl.BlockSpec(memory_space=pltpu.HBM),
         scratch_shapes=[pltpu.VMEM(a.shape, a.dtype) for a in args]
@@ -407,8 +403,6 @@
             chunk,
             chunk,
             chunk,
-            chunk,
-            rows,
             pltpu.VMEM((W, B * W), jnp.bfloat16),
             pltpu.VMEM((B * W, W), jnp.bfloat16),
             states,
@@ -419,13 +413,25 @@
             pltpu.VMEM((LEVELS - len(EARLY), PAIRS, 2 * ROWS, W), jnp.bfloat16),
             pltpu.SemaphoreType.DMA((len(args),)),
             pltpu.SemaphoreType.DMA((3,)),
-            pltpu.SemaphoreType.DMA((3,)),
+            pltpu.SemaphoreType.DMA((2,)),
+            pltpu.SemaphoreType.DMA((PARTS // TURN_ND,)),
             pltpu.SemaphoreType.DMA,
         ],
         compiler_params=pltpu.CompilerParams(
             has_side_effects=True, collective_id=0, vmem_limit_bytes=62 * 2**20
         ),
     )(*args)
+    blocks = 4
+    out = pl.pallas_call(
+        unpack_kernel,
+        grid=(blocks,),
+        out_shape=jax.ShapeDtypeStruct((2 * lines, W), jnp.float32),
+        in_specs=[
+            pl.BlockSpec((2, half // blocks, E, W), lambda i: (0, i, 0, 0)),
+            pl.BlockSpec((lines // blocks, W), lambda i: (i, 0)),
+        ],
+        out_specs=pl.BlockSpec((2 * lines // blocks, W), lambda i: (i, 0)),
+    )(field.reshape(2, half, E, W), target_order.reshape(lines, W))
     return out.reshape(lines, 2, W).transpose(1, 0, 2).reshape(2, lines * W)
 
 

time: 55.1 us -> 52.3 us (0.949)
  local copies, waits for them, and re-layouts: 1.87 us -> 0 us
  Pallas kernels: 53.1 us -> 52 us
    pallas_call x1, Pallas kernels: 53.1 us -> 48.6 us  [on_device(): pl.pallas_call(functools.partial(kernel, narrow), out_shape=jax.ShapeDtyp...]
    pallas_call x0 -> x1, Pallas kernels: none -> 3.46 us  [on_device(): pl.pallas_call(unpack_kernel, grid=(blocks,), out_shape=jax.ShapeDtypeStr...]
    unnamed x1 -> x0, local copies, waits for them, and re-layouts: 1.87 us -> none
where the time goes in v4:
time: 52.3 us; the launch traced here: 52 us
  Pallas kernels  52 us (99%)
    pallas_call x1, Pallas kernels, on_device(): pl.pallas_call(functools.partial(kernel, narrow), out_shape=jax.ShapeDtyp...  48.6 us
    pallas_call x1, Pallas kernels, on_device(): pl.pallas_call(unpack_kernel, grid=(blocks,), out_shape=jax.ShapeDtypeStr...  3.46 us

profile of v4, /device:TPU:1, one launch (start us, length us, event | category | flops | bytes accessed | tf_op | source)
XLA Modules:
  0.0 52.0 jit_solution(13701040644991905302)
XLA Ops:
  0.0 48.6 %shard_map.82 = bf16[128,8,128]{2,1,0:T(8,128)(2,1)} custom-call(f32[1024,128]{1,0:T(8,128)} %bitcast.16, s32[512,128]{1,0:T(8,128)} %bitcast.18, bf16[64,128]{1,0:T(8,128)(2,1)} %bitcast.19, bf16[16,128]{1,0:T(8,128)(2,1)} %leaf_hbm.1, bf16[10,2,2,128,128]{4,3,2,1,0:T(8,128)(2,1)} %mixing_hbm.1, bf16[16,128]{1,0:T(8,128)(2,1)} %bitcast.20, ...), custom_call_target="tpu_custom_call" | custom-call | tf_op jit(solution)/shard_map/pallas_call | solution.py:394
  48.6 3.5 %shard_map.83 = f32[1024,128]{1,0:T(8,128)} custom-call(bf16[2,64,8,128]{3,2,1,0:T(8,128)(2,1)} %bitcast.15, s32[512,128]{1,0:T(8,128)} %bitcast.17), custom_call_target="tpu_custom_call" | custom-call | tf_op jit(solution)/shard_map/pallas_call | solution.py:425

commit v5 on v4

--- a/solution.py
+++ b/solution.py
@@ -128,7 +128,7 @@
     return both.reshape(2 * rows, W)
 
 
-TURN_ND, FIRST_ND, LATER_PAIRS, LAST_ND = 8, 64, 2, 16
+TURN_ND, FIRST_ND, LATER_PAIRS, LAST_ND = 16, 128, 2, 32
 PAIRS = B // 2
 ROWS = PARTS * E
 EARLY = {0: 0, 1: 1, LEVELS - 1: 2}
@@ -421,7 +421,7 @@
             has_side_effects=True, collective_id=0, vmem_limit_bytes=62 * 2**20
         ),
     )(*args)
-    blocks = 4
+    blocks = 2
     out = pl.pallas_call(
         unpack_kernel,
         grid=(blocks,),

time: 52.3 us -> 47 us (0.90)
  Pallas kernels: 52 us -> 46.8 us
    pallas_call x1, Pallas kernels: 48.6 us -> 44.6 us  [on_device(): pl.pallas_call(functools.partial(kernel, narrow), out_shape=jax.ShapeDtyp...]
    pallas_call x1, Pallas kernels: 3.46 us -> 2.19 us  [on_device(): pl.pallas_call(unpack_kernel, grid=(blocks,), out_shape=jax.ShapeDtypeStr...]
where the time goes in v5:
time: 47 us; the launch traced here: 46.8 us
  Pallas kernels  46.8 us (100%)
    pallas_call x1, Pallas kernels, on_device(): pl.pallas_call(functools.partial(kernel, narrow), out_shape=jax.ShapeDtyp...  44.6 us
    pallas_call x1, Pallas kernels, on_device(): pl.pallas_call(unpack_kernel, grid=(blocks,), out_shape=jax.ShapeDtypeStr...  2.19 us

profile of v5, /device:TPU:1, one launch (start us, length us, event | category | flops | bytes accessed | tf_op | source)
XLA Modules:
  0.0 46.8 jit_solution(3210747933358753404)
XLA Ops:
  0.0 44.6 %shard_map.82 = bf16[128,8,128]{2,1,0:T(8,128)(2,1)} custom-call(f32[1024,128]{1,0:T(8,128)} %bitcast.16, s32[512,128]{1,0:T(8,128)} %bitcast.18, bf16[64,128]{1,0:T(8,128)(2,1)} %bitcast.19, bf16[16,128]{1,0:T(8,128)(2,1)} %leaf_hbm.1, bf16[10,2,2,128,128]{4,3,2,1,0:T(8,128)(2,1)} %mixing_hbm.1, bf16[16,128]{1,0:T(8,128)(2,1)} %bitcast.20, ...), custom_call_target="tpu_custom_call" | custom-call | tf_op jit(solution)/shard_map/pallas_call | solution.py:394
  44.7 2.2 %shard_map.83 = f32[1024,128]{1,0:T(8,128)} custom-call(bf16[2,64,8,128]{3,2,1,0:T(8,128)(2,1)} %bitcast.15, s32[512,128]{1,0:T(8,128)} %bitcast.17), custom_call_target="tpu_custom_call" | custom-call | tf_op jit(solution)/shard_map/pallas_call | solution.py:425

commit v6 on v5

--- a/solution.py
+++ b/solution.py
@@ -128,7 +128,7 @@
     return both.reshape(2 * rows, W)
 
 
-TURN_ND, FIRST_ND, LATER_PAIRS, LAST_ND = 16, 128, 2, 32
+TURN_ND, FIRST_ND, LATER_PAIRS, LAST_ND = 16, 128, 4, 32
 PAIRS = B // 2
 ROWS = PARTS * E
 EARLY = {0: 0, 1: 1, LEVELS - 1: 2}

time: 47 us -> 45.3 us (0.964)
  Pallas kernels: 46.8 us -> 45.1 us
    pallas_call x1, Pallas kernels: 44.6 us -> 42.9 us  [on_device(): pl.pallas_call(functools.partial(kernel, narrow), out_shape=jax.ShapeDtyp...]
where the time goes in v6:
time: 45.3 us; the launch traced here: 45.1 us
  Pallas kernels  45.1 us (100%)
    pallas_call x1, Pallas kernels, on_device(): pl.pallas_call(functools.partial(kernel, narrow), out_shape=jax.ShapeDtyp...  42.9 us
    pallas_call x1, Pallas kernels, on_device(): pl.pallas_call(unpack_kernel, grid=(blocks,), out_shape=jax.ShapeDtypeStr...  2.19 us

profile of v6, /device:TPU:1, one launch (start us, length us, event | category | flops | bytes accessed | tf_op | source)
XLA Modules:
  0.0 45.1 jit_solution(11760566154459065115)
XLA Ops:
  0.0 42.9 %shard_map.82 = bf16[128,8,128]{2,1,0:T(8,128)(2,1)} custom-call(f32[1024,128]{1,0:T(8,128)} %bitcast.16, s32[512,128]{1,0:T(8,128)} %bitcast.18, bf16[64,128]{1,0:T(8,128)(2,1)} %bitcast.19, bf16[16,128]{1,0:T(8,128)(2,1)} %leaf_hbm.1, bf16[10,2,2,128,128]{4,3,2,1,0:T(8,128)(2,1)} %mixing_hbm.1, bf16[16,128]{1,0:T(8,128)(2,1)} %bitcast.20, ...), custom_call_target="tpu_custom_call" | custom-call | tf_op jit(solution)/shard_map/pallas_call | solution.py:394
  42.9 2.2 %shard_map.83 = f32[1024,128]{1,0:T(8,128)} custom-call(bf16[2,64,8,128]{3,2,1,0:T(8,128)(2,1)} %bitcast.15, s32[512,128]{1,0:T(8,128)} %bitcast.17), custom_call_target="tpu_custom_call" | custom-call | tf_op jit(solution)/shard_map/pallas_call | solution.py:425

commit v7 on v6

--- a/solution.py
+++ b/solution.py
@@ -128,7 +128,7 @@
     return both.reshape(2 * rows, W)
 
 
-TURN_ND, FIRST_ND, LATER_PAIRS, LAST_ND = 16, 128, 4, 32
+TURN_ND, FIRST_ND, LATER_PAIRS, LAST_ND = 32, 128, 4, 32
 PAIRS = B // 2
 ROWS = PARTS * E
 EARLY = {0: 0, 1: 1, LEVELS - 1: 2}

time: 45.3 us -> 44.4 us (0.980)
  Pallas kernels: 45.1 us -> 44.2 us
    pallas_call x1, Pallas kernels: 42.9 us -> 42 us  [on_device(): pl.pallas_call(functools.partial(kernel, narrow), out_shape=jax.ShapeDtyp...]
where the time goes in v7:
time: 44.4 us; the launch traced here: 44.2 us
  Pallas kernels  44.2 us (100%)
    pallas_call x1, Pallas kernels, on_device(): pl.pallas_call(functools.partial(kernel, narrow), out_shape=jax.ShapeDtyp...  42 us
    pallas_call x1, Pallas kernels, on_device(): pl.pallas_call(unpack_kernel, grid=(blocks,), out_shape=jax.ShapeDtypeStr...  2.19 us

profile of v7, /device:TPU:1, one launch (start us, length us, event | category | flops | bytes accessed | tf_op | source)
XLA Modules:
  0.0 44.2 jit_solution(9212917606723538413)
XLA Ops:
  0.0 42.0 %shard_map.82 = bf16[128,8,128]{2,1,0:T(8,128)(2,1)} custom-call(f32[1024,128]{1,0:T(8,128)} %bitcast.16, s32[512,128]{1,0:T(8,128)} %bitcast.18, bf16[64,128]{1,0:T(8,128)(2,1)} %bitcast.19, bf16[16,128]{1,0:T(8,128)(2,1)} %leaf_hbm.1, bf16[10,2,2,128,128]{4,3,2,1,0:T(8,128)(2,1)} %mixing_hbm.1, bf16[16,128]{1,0:T(8,128)(2,1)} %bitcast.20, ...), custom_call_target="tpu_custom_call" | custom-call | tf_op jit(solution)/shard_map/pallas_call | solution.py:394
  42.0 2.2 %shard_map.83 = f32[1024,128]{1,0:T(8,128)} custom-call(bf16[2,64,8,128]{3,2,1,0:T(8,128)(2,1)} %bitcast.15, s32[512,128]{1,0:T(8,128)} %bitcast.17), custom_call_target="tpu_custom_call" | custom-call | tf_op jit(solution)/shard_map/pallas_call | solution.py:425
